TPU v7x, 512 devices: a whole 4x8x8 slice. The times are simulated.
512 devices in a mesh: dev: 128 (over x, z_lo, y, core), rep: 4 (over z_hi).
Axes of the slice: x: 4, y: 8, z: 8 (z_hi: 4, z_lo: 2; z = z_hi * 2 + z_lo), core: 2. Of those that a mesh axis runs over, the one named last changes fastest.
Arguments:
- backbone: bfloat16 [512, 16, 8, 512], P(('rep', 'dev')), parts along dimension 0, may hold values from -6 to 6
- conv_weight: bfloat16 [3, 3, 512, 2048], P(None, None, None, ('rep', 'dev')), parts along dimension 3, may hold values from -0.35355339 to 0.35355339
- smooth_weight: float32 [3, 3, 2048], P(None, None, 'rep'), parts along dimension 2, may hold values from -2.5 to 2.5
Outputs:
- smoothed: bfloat16 [512, 16, 8, 512], P(('rep', 'dev')), parts along dimension 0
There are 4 independent parts, one for each index of `rep`. A program takes and returns all parts, laid end to end along the dimension named above; each array names one. Nothing has to cross between parts.
All inputs are finite; a program needn't handle non-finite values.
Results may differ from a plain program's by a relative error of at most 0.0073.
Values may be sent and summed in bfloat16 or wider, within the bound.
No kernel may reach another device: no remote copies, remote signals or barrier semaphores. Data moves between devices by JAX's collectives and lax.ppermute only.
A program may use at most 64 MiB of HBM per device.

v0:
```python
import jax
import jax.numpy as jnp
from jax import lax
from jax.sharding import PartitionSpec as P

ITERS = 2


ridge_term = 0.5


def convolve(padded, weights, grid_rows, grid_cols):
    summed = None
    for row_tap in range(3):
        for col_tap in range(3):
            window = padded[:, row_tap : row_tap + grid_rows, col_tap : col_tap + grid_cols, :]
            flat_window = window.reshape(-1, window.shape[3])
            product = jnp.dot(
                flat_window, weights[row_tap, col_tap], preferred_element_type=jnp.float32
            )
            summed = product if summed is None else summed + product
    return summed.reshape(padded.shape[0], grid_rows, grid_cols, weights.shape[3])


def single_root(moments):
    identity = jnp.eye(moments.shape[0], dtype=jnp.float32)
    frob = jnp.sqrt(jnp.sum(moments * moments))
    upper = moments / frob
    lower = identity
    for sweep in range(ITERS):
        product = jnp.dot(lower, upper, precision=lax.Precision.HIGHEST)
        factor = 1.5 * identity - 0.5 * product
        if sweep + 1 < ITERS:
            upper = jnp.dot(upper, factor, precision=lax.Precision.HIGHEST)
        lower = jnp.dot(factor, lower, precision=lax.Precision.HIGHEST)
    return lower / jnp.sqrt(frob)


def whiten_block(received):
    features_block = received[:, 0]
    image_count = features_block.shape[0]
    channels = features_block.shape[2]
    identity = jnp.eye(channels, dtype=jnp.float32)
    center = jnp.sum(features_block.astype(jnp.float32), axis=0) / image_count
    centered = (features_block.astype(jnp.float32) - center).astype(jnp.bfloat16)
    gram = jnp.einsum("nkc,nkd->kcd", centered, centered, preferred_element_type=jnp.float32)
    moments = gram / (image_count - 1) + ridge_term * identity
    roots = lax.map(single_root, moments)
    roots = roots.astype(jnp.bfloat16)
    whitened = jnp.einsum(
        "nkc,kcd->nkd", centered, roots, preferred_element_type=jnp.float32
    ).astype(jnp.bfloat16)
    return whitened[:, None]


def shards(backbone, conv_weight, smooth_weight):
    local_images = backbone.shape[0]
    grid_rows = backbone.shape[1]
    grid_cols = backbone.shape[2]
    channels = backbone.shape[3]
    owners = lax.axis_size("dev")
    padded = jnp.pad(backbone, ((0, 0), (1, 1), (1, 1), (0, 0)))
    kernel = lax.all_gather(conv_weight, "dev", axis=3, tiled=True)
    conv_out = convolve(padded, kernel, grid_rows, grid_cols)
    per_owner = grid_rows * grid_cols // owners
    features = conv_out.astype(jnp.bfloat16).reshape(local_images, owners, per_owner, channels)
    whitened = whiten_block(
        lax.all_to_all(features, "dev", split_axis=1, concat_axis=0, tiled=True)
    )
    returned = lax.all_to_all(whitened, "dev", split_axis=0, concat_axis=1, tiled=True)
    returned = returned.reshape(local_images, grid_rows, grid_cols, channels)
    padded_white = jnp.pad(returned, ((0, 0), (1, 1), (1, 1), (0, 0)))
    summed = jnp.zeros((local_images, grid_rows, grid_cols, channels), jnp.float32)
    for row_tap in range(3):
        for col_tap in range(3):
            window = padded_white[
                :, row_tap : row_tap + grid_rows, col_tap : col_tap + grid_cols, :
            ]
            summed = summed + window.astype(jnp.float32) * smooth_weight[row_tap, col_tap]
    return summed.astype(jnp.bfloat16)


def solution(mesh):
    placed = (
        P(("rep", "dev"), None, None, None),
        P(None, None, None, ("rep", "dev")),
        P(None, None, "rep"),
    )
    return jax.shard_map(
        shards,
        mesh=mesh,
        in_specs=placed,
        out_specs=P(("rep", "dev"), None, None, None),
        check_vma=False,
    )
```

profile of v0, /device:TPU:1, one launch (start us, length us, event | category | flops | bytes accessed | tf_op | source)
XLA Modules:
  0.0 345.1 jit_solution(14790321609987311031)
XLA Ops:
  6.5 1.4 copy.10
  8.0 225.6 %all-gather.2.cloned.1.call-done = bf16[3,3,512,512]{2,1,0,3:T(4,128)(2,1)} async-done(((bf16[3,3,512,4]{2,1,0,3:T(4,128)(2,1)}), bf16[3,3,512,512]{2,1,0,3:T(4,128)(2,1)}) %all-gather.2.cloned.1.call-update) | async-done | bytes 4718608 | tf_op jit(solution)/shard_map/all_gather | solution.py:63
  233.5 13.9 %fusion.48 = (bf16[1,1,512,512]{2,1,0,3:T(2,128)(2,1)S(1)}, bf16[1,1,512,512]{2,1,0,3:T(2,128)(2,1)S(1)}, bf16[1,1,512,512]{2,1,0,3:T(2,128)(2,1)S(1)}, bf16[1,1...) fusion(bf16[3,3,512,512]{2,1,0,3:T(4,128)(2,1)} %all-gather.2.c, ...), kind=kLoop, calls=%fused_computation.79 | loop fusion | bytes 9437184 | tf_op jit(solution)/shard_map/slice | solution.py:19
  247.5 3.5 %copy.25 = bf16[1,1,512,512]{3,2,1,0:T(8,128)(2,1)} copy(bf16[1,1,512,512]{2,1,0,3:T(2,128)(2,1)} %get-tuple-element.22) | data formatting | bytes 1048576
  250.9 3.5 %copy.26 = bf16[1,1,512,512]{3,2,1,0:T(8,128)(2,1)} copy(bf16[1,1,512,512]{2,1,0,3:T(2,128)(2,1)} %get-tuple-element.21) | data formatting | bytes 1048576
  254.5 3.5 %copy.27 = bf16[1,1,512,512]{3,2,1,0:T(8,128)(2,1)} copy(bf16[1,1,512,512]{2,1,0,3:T(2,128)(2,1)} %get-tuple-element.20) | data formatting | bytes 1048576
  258.0 3.5 %copy.28 = bf16[1,1,512,512]{3,2,1,0:T(8,128)(2,1)} copy(bf16[1,1,512,512]{2,1,0,3:T(2,128)(2,1)} %get-tuple-element.19) | data formatting | bytes 1048576
  261.5 3.5 %copy.29 = bf16[1,1,512,512]{3,2,1,0:T(8,128)(2,1)} copy(bf16[1,1,512,512]{2,1,0,3:T(2,128)(2,1)} %get-tuple-element.18) | data formatting | bytes 1048576
  265.0 3.5 %copy.30 = bf16[1,1,512,512]{3,2,1,0:T(8,128)(2,1)} copy(bf16[1,1,512,512]{2,1,0,3:T(2,128)(2,1)} %get-tuple-element.17) | data formatting | bytes 1048576
  268.5 2.3 copy.31
  270.7 1.3 copy.32
  272.1 1.3 copy.33
  273.4 1.3 fusion.14
  274.7 1.3 convolution_add_fusion.7
  276.0 1.3 convolution_add_fusion.6
  277.2 1.3 convolution_add_fusion.5
  278.5 1.3 convolution_add_fusion.4
  281.0 0.5 broadcast.75
  281.5 1.4 reduce.2
  282.9 24.3 %all_to_all.8 = bf16[128,2,256]{2,1,0:T(2,128)(2,1)S(1)} all-to-all(bf16[128,2,256]{2,1,0:T(2,128)(2,1)S(1)} %reshape.207), channel_id=1, replica_groups=mesh['dev'=128,'rep'=4] {'dev'}, dimensions={0} | all-to-all | bytes 262144 | tf_op jit(solution)/shard_map/all_to_all | solution.py:68
  308.0 1.1 multiply_reduce_fusion
  309.6 1.1 select_subtract_fusion.1
  310.7 1.9 fusion.16
  312.6 1.0 fusion.5
  313.9 1.9 select_subtract_fusion
  315.8 1.8 fusion.1
  317.7 0.3 fusion.3
  318.0 0.7 reduce.3
  318.8 0.7 reshape.209
  319.5 5.6 %all-to-all-start.1 = ((bf16[128,2,256]{2,1,0:T(2,128)(2,1)}), bf16[128,2,256]{2,1,0:T(2,128)(2,1)S(1)}, u32[]{:S(2)}, u32[]{:S(2)}) async-start(bf16[128,2,256]{2,1,0:T(2,128)(2,1)} %reshape.209), calls=%async_computation.1 | async-start | bytes 262144 | tf_op jit(solution)/shard_map/all_to_all | solution.py:70
  325.1 12.2 %all-to-all-done.1 = bf16[128,2,256]{2,1,0:T(2,128)(2,1)S(1)} async-done(((bf16[128,2,256]{2,1,0:T(2,128)(2,1)}), bf16[128,2,256]{2,1,0:T(2,128)(2,1)S(1)}, u32[]{:S(2)}, u32[]{:S(2)}) %all-to-all-start.1) | async-done | bytes 131104 | tf_op jit(solution)/shard_map/all_to_all | solution.py:70
  337.4 0.9 add_convert_fusion
  (25 shorter events, 2.4 us)
Async XLA Ops:
  6.5 227.0 %all-gather.2.cloned.1.call-start = ((), (), s32[]{:S(2)}) async-start(), calls=%async_computation.2 | async-start | bytes 6340608 | tf_op jit(solution)/shard_map/all_gather | solution.py:63
  250.9 22.4 %copy-start = (bf16[1,16,8,512]{3,2,1,0:T(8,128)(2,1)S(1)}, bf16[1,16,8,512]{3,2,1,0:T(8,128)(2,1)}, u32[]{:S(2)}) copy-start(bf16[1,16,8,512]{3,2,1,0:T(8,128)(2,1)} %param.3) | copy-start | bytes 393220
  270.7 9.3 %copy-start.1 = (bf16[1,1,512,512]{3,2,1,0:T(8,128)(2,1)S(1)}, bf16[1,1,512,512]{3,2,1,0:T(8,128)(2,1)}, u32[]{:S(2)}) copy-start(bf16[1,1,512,512]{3,2,1,0:T(8,128)(2,1)} %copy.31) | copy-start | bytes 1572868
  272.0 7.7 %copy-start.2 = (bf16[1,1,512,512]{3,2,1,0:T(8,128)(2,1)S(1)}, bf16[1,1,512,512]{3,2,1,0:T(8,128)(2,1)}, u32[]{:S(2)}) copy-start(bf16[1,1,512,512]{3,2,1,0:T(8,128)(2,1)} %copy.30) | copy-start | bytes 1572868
  312.6 12.5 %copy-start.3 = (f32[3,3,512]{2,1,0:T(4,128)S(1)}, f32[3,3,512]{2,1,0:T(4,128)}, u32[]{:S(2)}) copy-start(f32[3,3,512]{2,1,0:T(4,128)} %param.5) | copy-start | bytes 55300
  319.5 17.8 %all-to-all-start.1 = ((bf16[128,2,256]{2,1,0:T(2,128)(2,1)}), bf16[128,2,256]{2,1,0:T(2,128)(2,1)S(1)}, u32[]{:S(2)}, u32[]{:S(2)}) async-start(bf16[128,2,256]{2,1,0:T(2,128)(2,1)} %reshape.209), calls=%async_computation.1 | async-start | bytes 262144 | tf_op jit(solution)/shard_map/all_to_all | solution.py:70
Sparse Core Ops, SparseCore 0:
  9.5 224.0 all-gather.1
where the time goes:
time: 346 us; the launch traced here: 345 us
  waiting for transfers between devices  238 us (69%)
  local copies, waits for them, and re-layouts  43 us (12%)
  blocking collectives  24.3 us (7%)
  matrix products  16.3 us (5%)
  between operations  14.3 us (4%)
  starting transfers between devices  5.56 us (2%)
  other arithmetic  3.8 us (1%)
    all_gather x1, waiting for transfers between devices, shards(): kernel = lax.all_gather(conv_weight, 'dev', axis=3, tiled=True)  226 us
    unnamed x25, local copies, waits for them, and re-layouts  28.9 us
    all_to_all x1, blocking collectives, shards(): lax.all_to_all(features, 'dev', split_axis=1, concat_axis=0, tiled=True)  24.3 us
    slice x1, local copies, waits for them, and re-layouts, convolve(): weights[row_tap, col_tap]  13.9 us
    all_to_all x1, waiting for transfers between devices, shards(): lax.all_to_all(whitened, 'dev', split_axis=0, concat_axis=1, tiled=True)  12.2 us
    dot_general x9, matrix products, convolve(): jnp.dot(flat_window, weights[row_tap, col_tap], preferred_element_type=jn...  7.3 us
  transfers between devices with their start and end apart: 2, of which 2 were waited for; matrix products, arithmetic and copies ran while one was open for 0% of the time, Pallas kernels for 0%

commit v1 on v0

v1 whole, which is shorter than its diff:
```python
import numpy as np
import jax
import jax.numpy as jnp
from jax import lax
from jax.experimental import pallas as pl
from jax.experimental.pallas import tpu as pltpu
from jax.sharding import Mesh, PartitionSpec as P

ITERS = 2
RIDGE = 0.5
NX, NZ, NY, NC = 4, 2, 8, 2
ROWS, COLS, CH, IMAGES = 16, 8, 512, 128
F32, BF16 = jnp.float32, jnp.bfloat16
AXES = ("x", "z", "y", "c")
NT = (((1,), (1,)), ((), ()))


def vmem_call(body, out_shape, scratch, name):
    return pl.pallas_call(
        body,
        out_shape=out_shape,
        scratch_shapes=scratch,
        name=name,
        compiler_params=pltpu.CompilerParams(vmem_limit_bytes=48 * 1024 * 1024),
    )


def interleave_body(own_ref, partner_ref, out_ref, rows_ref):
    for t in range(4):
        lanes = slice(t * 128, (t + 1) * 128)
        for j in range(4):
            rows_ref[t, pl.ds(j, IMAGES, stride=8), :] = own_ref[j, :, lanes].astype(F32)
            rows_ref[t, pl.ds(4 + j, IMAGES, stride=8), :] = partner_ref[j, :, lanes].astype(F32)
        out_ref[:, lanes] = rows_ref[t].astype(BF16)


def conv_body(weight_ref, x_ref, out_ref, wide_ref, z_ref):
    taps, group = weight_ref.shape[1], weight_ref.shape[0]
    for t in range(taps):
        for g in range(group):
            at = t * 64 + g * 4
            wide_ref[at : at + 4, :] = weight_ref[g, t].astype(F32)
    wide_ref[576:640, :] = jnp.zeros((64, CH), F32)
    z_ref[0] = jnp.zeros((10, 8, 640), F32)
    z_ref[17] = jnp.zeros((10, 8, 640), F32)
    z_ref[:, 0] = jnp.zeros((18, 8, 640), F32)
    z_ref[:, 9] = jnp.zeros((18, 8, 640), F32)
    x = x_ref[...]
    for lo, hi in ((0, 256), (256, 512), (512, 640)):
        part = lax.dot_general(x, wide_ref[lo:hi, :].astype(BF16), NT, preferred_element_type=F32)
        z_ref[1:17, 1:9, :, lo:hi] = part.reshape(ROWS, COLS, 8, hi - lo)
    lane_lo = lax.broadcasted_iota(jnp.int32, (4, 8, 128), 2) < 64
    row_lo = lax.broadcasted_iota(jnp.int32, (4, 8, 128), 1) < 4
    for h in range(ROWS):
        sums = [None, None]
        for t in range(taps):
            a, b, tile = t // 3, t % 3, (t // 2) * 128
            piece = z_ref[h + a, b : b + 8, :, tile : tile + 128]
            sums[t % 2] = piece if sums[t % 2] is None else sums[t % 2] + piece
        total = sums[0] + pltpu.roll(sums[1], 64, 2)
        pairs = total.reshape(4, 2, 8, 128)
        even, odd = pairs[:, 0], pairs[:, 1]
        first = jnp.where(row_lo, even, pltpu.roll(odd, 4, 1))
        second = jnp.where(row_lo, pltpu.roll(even, 4, 1), odd)
        packed = jnp.where(lane_lo, first, pltpu.roll(second, 64, 2))
        out_ref[h * 32 : (h + 1) * 32, :] = packed.reshape(32, 128).astype(BF16)


def exact_dot(a, b):
    return jnp.dot(a, b, precision=lax.Precision.HIGHEST, preferred_element_type=F32)


def stats_body(got_ref, pick_ref, lanes_ref, out_ref, rows_ref):
    lane_lo = lax.broadcasted_iota(jnp.int32, (IMAGES, 128), 1) < 64
    even_row = lax.broadcasted_iota(jnp.int32, (IMAGES, 128), 0) % 2 == 0
    eye = (
        lax.broadcasted_iota(jnp.int32, (IMAGES, IMAGES), 0)
        == lax.broadcasted_iota(jnp.int32, (IMAGES, IMAGES), 1)
    ).astype(F32)
    centered = []
    gram = None
    for k in range(NX):
        block = got_ref[k * 128 : (k + 1) * 128, :]
        from0 = jnp.dot(pick_ref[2 * k], block, preferred_element_type=F32)
        from1 = jnp.dot(pick_ref[2 * k + 1], block, preferred_element_type=F32)
        same = jnp.where(lane_lo, from0, from1)
        swapped = pltpu.roll(jnp.where(lane_lo, from1, from0), 64, 1)
        mixed = jnp.where(even_row, same, swapped).astype(BF16)
        x = jnp.dot(mixed, lanes_ref[...], preferred_element_type=F32)
        center = jnp.sum(x, axis=0, keepdims=True) / IMAGES
        x = (x - center).astype(BF16)
        centered.append(x)
        part = lax.dot_general(x, x, NT, preferred_element_type=F32)
        gram = part if gram is None else gram + part
    scaled = gram / (IMAGES - 1)
    trace = jnp.sum(scaled * eye)
    frob = jnp.sqrt(jnp.sum(scaled * scaled) + 2.0 * RIDGE * trace + RIDGE * RIDGE * CH)
    upper = (scaled + RIDGE * eye) / frob
    lower = 1.5 * eye - 0.5 * upper
    upper = exact_dot(upper, lower)
    for sweep in range(1, ITERS):
        factor = 1.5 * eye - 0.5 * exact_dot(lower, upper)
        if sweep + 1 < ITERS:
            upper = exact_dot(upper, factor)
        lower = exact_dot(factor, lower)
    lower = lower / jnp.sqrt(frob)
    high = lower.astype(BF16)
    low = (lower - high.astype(F32)).astype(BF16)
    for k in range(NX):
        white = jnp.dot(high, centered[k], preferred_element_type=F32)
        white = white + jnp.dot(low, centered[k], preferred_element_type=F32)
        rows_ref[pl.ds(k, IMAGES, stride=4), :] = white
    out_ref[...] = rows_ref[...].astype(BF16)


def smooth_body(white_ref, weight_ref, out_ref, pad_ref, rows_ref):
    pad_ref[...] = jnp.zeros((18, 40, 128), F32)
    pad_ref[1:17, 4:36, :] = white_ref[...].astype(F32).reshape(ROWS, 32, 128)
    total = None
    for t in range(9):
        a, b = t // 3, t % 3
        piece = pad_ref[a : a + ROWS, 4 * b : 4 * b + 32, :] * weight_ref[t][None]
        total = piece if total is None else total + piece
    rows_ref[...] = total.reshape(512, 128)
    for k in range(NX):
        out_ref[:, k * 128 : (k + 1) * 128] = rows_ref[pl.ds(k, 128, stride=4), :].astype(BF16)


def pick_tables():
    picks = np.zeros((2 * NX, IMAGES, 128), np.float32)
    for x in range(NX):
        for c in range(NC):
            for n in range(IMAGES):
                xs, zy = n // 32, (n // 2) % 16
                picks[2 * x + c, n, zy * 8 + c * 4 + (x - xs) % NX] = 1.0
    lanes = np.zeros((128, 128), np.float32)
    for c in range(NC):
        for zy in range(16):
            for k in range(4):
                lanes[c * 64 + zy * 4 + k, zy * 8 + c * 4 + k] = 1.0
    return picks, lanes


PICKS, LANES = pick_tables()


def shards(backbone, conv_weight, smooth_weight):
    image = backbone.reshape(ROWS * COLS, CH)
    chunk = conv_weight.transpose(0, 1, 3, 2).reshape(9, 4, CH)
    spread = jnp.broadcast_to(chunk[None], (NZ * NY, 9, 4, CH))
    kernels = lax.all_to_all(spread, ("z", "y"), 0, 0, tiled=True)
    own = [image]
    for k in range(1, NX):
        own.append(lax.ppermute(image, "x", [(i, (i + k) % NX) for i in range(NX)]))
    own = jnp.stack(own)
    partner = lax.ppermute(own, "c", [(0, 1), (1, 0)])
    x = vmem_call(
        interleave_body,
        jax.ShapeDtypeStruct((1024, CH), BF16),
        [pltpu.VMEM((4, 1024, 128), F32)],
        "interleave",
    )(own, partner)
    features = vmem_call(
        conv_body,
        jax.ShapeDtypeStruct((512, 128), BF16),
        [pltpu.VMEM((640, CH), F32), pltpu.VMEM((18, 10, 8, 640), F32)],
        "conv",
    )(kernels, x)
    got = lax.all_to_all(features.reshape(128, 4, 128), AXES, 0, 0, tiled=True)
    white = vmem_call(
        stats_body,
        jax.ShapeDtypeStruct((512, 128), BF16),
        [pltpu.VMEM((512, 128), F32)],
        "stats",
    )(got.reshape(512, 128), jnp.asarray(PICKS, BF16), jnp.asarray(LANES, BF16))
    back = lax.all_to_all(white.reshape(128, 4, 128), AXES, 0, 0, tiled=True)
    taps = jnp.tile(smooth_weight.reshape(9, 4, 128), (1, 8, 1))
    out = vmem_call(
        smooth_body,
        jax.ShapeDtypeStruct((128, CH), BF16),
        [pltpu.VMEM((18, 40, 128), F32), pltpu.VMEM((512, 128), F32)],
        "smooth",
    )(back.reshape(512, 128), taps)
    return out.reshape(1, ROWS, COLS, CH)


def solution(mesh):
    split = Mesh(
        mesh.devices.reshape(NX, NZ, NY, NC, mesh.shape["rep"]), AXES + ("rep",)
    )
    whole = ("rep",) + AXES
    return jax.shard_map(
        shards,
        mesh=split,
        in_specs=(P(whole, None, None, None), P(None, None, None, whole), P(None, None, "rep")),
        out_specs=P(whole, None, None, None),
        check_vma=False,
    )
```

time: 346 us -> 79 us (0.23)
  waiting for transfers between devices: 238 us -> 16.5 us
  local copies, waits for them, and re-layouts: 43 us -> 1.79 us
  starting transfers between devices: 5.56 us -> 30.4 us
  matrix products: 16.3 us -> 0 us
  between operations: 14.3 us -> 0.12 us
  Pallas kernels: 0 us -> 5.81 us
  other arithmetic: 3.8 us -> 0.07 us
    all_gather x1 -> x0, waiting for transfers between devices: 226 us -> none  [shards(): kernel = lax.all_gather(conv_weight, 'dev', axis=3, tiled=True)]
    unnamed x25 -> x8, local copies, waits for them, and re-layouts: 28.9 us -> 0.02 us
    dot_general x16 -> x0, matrix products: 16.3 us -> none  [the longest x9 7.3 us: convolve(): jnp.dot(flat_window, weights[row_tap, col_tap], preferred_element_type=jn...]
    ppermute x0 -> x4, starting transfers between devices: none -> 15 us  [the longest x3 10.5 us: shards(): own.append(lax.ppermute(image, 'x', [(i, (i + k) % NX) for i in range(NX)]))]
    slice x2 -> x0, local copies, waits for them, and re-layouts: 13.9 us -> none  [the longest x1 13.9 us: convolve(): weights[row_tap, col_tap]]
    all_to_all x1 -> x2, starting transfers between devices: 5.56 us -> 15.4 us  [the longest x1 9.68 us: shards(): kernels = lax.all_to_all(spread, ('z', 'y'), 0, 0, tiled=True)]
    pallas_call x0 -> x4, Pallas kernels: none -> 5.81 us  [the longest x1 2.9 us: shards(): vmem_call(stats_body, jax.ShapeDtypeStruct((512, 128), BF16), [pltpu.VMEM...]
    ppermute x0 -> x4, waiting for transfers between devices: none -> 4.27 us  [the longest x3 2.75 us: shards(): own.append(lax.ppermute(image, 'x', [(i, (i + k) % NX) for i in range(NX)]))]
  transfers between devices with their start and end apart: 2 -> 6, of which waited for: 2 -> 4; matrix products, arithmetic and copies ran while one was open for 0% -> 0% of each run, Pallas kernels for 0% -> 1%
where the time goes in v1:
time: 79 us; the launch traced here: 78.5 us
  starting transfers between devices  30.4 us (38%)
  blocking collectives  23.8 us (30%)
  waiting for transfers between devices  16.5 us (21%)
  Pallas kernels  5.81 us (7%)
  local copies, waits for them, and re-layouts  1.79 us (2%)
    all_to_all x1, blocking collectives, shards(): got = lax.all_to_all(features.reshape(128, 4, 128), AXES, 0, 0, tiled=True)  23.8 us
    all_to_all x1, waiting for transfers between devices, shards(): back = lax.all_to_all(white.reshape(128, 4, 128), AXES, 0, 0, tiled=True)  12.2 us
    ppermute x3, starting transfers between devices, shards(): own.append(lax.ppermute(image, 'x', [(i, (i + k) % NX) for i in range(NX)]))  10.5 us
    all_to_all x1, starting transfers between devices, shards(): kernels = lax.all_to_all(spread, ('z', 'y'), 0, 0, tiled=True)  9.68 us
    all_to_all x1, starting transfers between devices, shards(): back = lax.all_to_all(white.reshape(128, 4, 128), AXES, 0, 0, tiled=True)  5.69 us
    ppermute x1, starting transfers between devices, shards(): partner = lax.ppermute(own, 'c', [(0, 1), (1, 0)])  4.45 us
    pallas_call x1, Pallas kernels, shards(): vmem_call(stats_body, jax.ShapeDtypeStruct((512, 128), BF16), [pltpu.VMEM...  2.9 us
    ppermute x3, waiting for transfers between devices, shards(): own.append(lax.ppermute(image, 'x', [(i, (i + k) % NX) for i in range(NX)]))  2.75 us
  transfers between devices with their start and end apart: 6, of which 4 were waited for; matrix products, arithmetic and copies ran while one was open for 0% of the time, Pallas kernels for 1%

profile of v1, /device:TPU:1, one launch (start us, length us, event | category | flops | bytes accessed | tf_op | source)
XLA Modules:
  0.0 78.5 jit_solution(8185141125212552928)
XLA Ops:
  0.0 1.7 %broadcast_in_dim.8 = bf16[16,9,4,512]{3,2,1,0:T(4,128)(2,1)} broadcast(bf16[9,4,512]{2,1,0:T(4,128)(2,1)} %bitcast.25), dimensions={1,2,3} | broadcast | bytes 626688 | tf_op jit(solution)/shard_map/broadcast_in_dim | solution.py:150
  1.7 0.0 copy-start.2
  1.7 9.7 %all-to-all-start = ((bf16[16,9,4,512]{3,2,1,0:T(4,128)(2,1)}), bf16[16,9,4,512]{3,2,1,0:T(4,128)(2,1)S(1)}, u32[]{:S(2)}, u32[]{:S(2)}) async-start(bf16[16,9,4,512]{3,2,1,0:T(4,128)(2,1)} %broadcast_in_dim.8), calls=%async_computation | async-start | bytes 1179648 | tf_op jit(solution)/shard_map/all_to_all | solution.py:151
  11.4 0.0 copy-done.2
  11.4 3.1 %collective-permute-start = (bf16[128,512]{1,0:T(8,128)(2,1)S(1)}, bf16[128,512]{1,0:T(8,128)(2,1)S(1)}, u32[]{:S(2)}, u32[]{:S(2)}) collective-permute-start(bf16[128,512]{1,0:T(8,128)(2,1)S(1)} %bitcast.18), channel_id=1, source_target_pairs={{0,128},{128,256},{256,384},{384,0},{1,129},{129,257},{257,385},{3... | collective-permute-start | bytes 393224 | tf_op jit(solution)/shard_map/ppermute | solution.py:154
  14.6 4.4 %collective-permute-start.1 = (bf16[128,512]{1,0:T(8,128)(2,1)S(1)}, bf16[128,512]{1,0:T(8,128)(2,1)S(1)}, u32[]{:S(2)}, u32[]{:S(2)}) collective-permute-start(bf16[128,512]{1,0:T(8,128)(2,1)S(1)} %bitcast.19), channel_id=1, source_target_pairs={{0,256},{128,384},{256,0},{384,128},{1,257},{129,385},{257,1},{385... | collective-permute-start | bytes 393224 | tf_op jit(solution)/shard_map/ppermute | solution.py:154
  18.9 3.1 %collective-permute-start.2 = (bf16[128,512]{1,0:T(8,128)(2,1)S(1)}, bf16[128,512]{1,0:T(8,128)(2,1)S(1)}, u32[]{:S(2)}, u32[]{:S(2)}) collective-permute-start(bf16[128,512]{1,0:T(8,128)(2,1)S(1)} %bitcast.20), channel_id=1, source_target_pairs={{0,384},{128,0},{256,128},{384,256},{1,385},{129,1},{257,129},{385... | collective-permute-start | bytes 393224 | tf_op jit(solution)/shard_map/ppermute | solution.py:154
  22.0 0.0 collective-permute-done
  22.0 0.5 collective-permute-done.1
  22.5 2.2 %collective-permute-done.2 = bf16[128,512]{1,0:T(8,128)(2,1)S(1)} collective-permute-done((bf16[128,512]{1,0:T(8,128)(2,1)S(1)}, bf16[128,512]{1,0:T(8,128)(2,1)S(1)}, u32[]{:S(2)}, u32[]{:S(2)}) %collective-permute-start.2) | collective-permute-done | bytes 131104 | tf_op jit(solution)/shard_map/ppermute | solution.py:154
  24.8 0.1 pad_maximum_fusion.own_ref
  24.8 4.5 %collective-permute-start.3 = (bf16[4,128,512]{2,1,0:T(8,128)(2,1)S(1)}, bf16[4,128,512]{2,1,0:T(8,128)(2,1)S(1)}, u32[]{:S(2)}, u32[]{:S(2)}) collective-permute-start(bf16[4,128,512]{2,1,0:T(8,128)(2,1)S(1)} %pad_maximum_fusion.own_ref), channel_id=1, source_target_pairs={{0,4},{4,0},{1,5},{5,1},{2,6},{6,2},{3,7},{7,3},{8,12},{12,8},{9,1... | collective-permute-start | bytes 1572872 | tf_op jit(solution)/shard_map/ppermute | solution.py:156
  29.3 1.5 %collective-permute-done.3.partner_ref = bf16[4,128,512]{2,1,0:T(8,128)(2,1)S(1)} collective-permute-done((bf16[4,128,512]{2,1,0:T(8,128)(2,1)S(1)}, bf16[4,128,512]{2,1,0:T(8,128)(2,1)S(1)}, u32[]{:S(2)}, u32[]{:S(2)}) %collective-permute-start.3) | collective-permute-done | bytes 524320 | tf_op jit(solution)/shard_map/ppermute | solution.py:156
  30.8 0.7 interleave.1.x_ref
  31.5 0.0 all-to-all-done.weight_ref
  31.5 0.0 copy-start.1
  31.5 1.3 %conv.1 = bf16[512,128]{1,0:T(8,128)(2,1)S(1)} custom-call(bf16[16,9,4,512]{3,2,1,0:T(4,128)(2,1)S(1)} %all-to-all-done.weight_ref, bf16[1024,512]{1,0:T(8,128)(2,1)S(1)} %interleave.1.x_ref), custom_call_target="tpu_custom_call" | custom-call | tf_op jit(solution)/shard_map/conv/pallas_call | solution.py:163
  32.8 0.0 copy-start
  32.8 23.8 %all_to_all.15 = bf16[128,4,128]{2,1,0:T(4,128)(2,1)S(1)} all-to-all(bf16[128,4,128]{2,1,0:T(4,128)(2,1)S(1)} %bitcast.17), channel_id=1, replica_groups=mesh['x'=4,'z'=2,'y'=8,'c'=2,'rep'=4] {'x','z','y','c'}, dimensions={0} | all-to-all | bytes 262144 | tf_op jit(solution)/shard_map/all_to_all | solution.py:169
  56.6 0.0 copy-done.1
  56.6 0.0 copy-done
  56.6 2.9 %stats.1 = bf16[512,128]{1,0:T(8,128)(2,1)} custom-call(bf16[512,128]{1,0:T(8,128)(2,1)S(1)} %bitcast.16, bf16[8,128,128]{2,1,0:T(8,128)(2,1)S(1)} %copy-done, bf16[128,128]{1,0:T(8,128)(2,1)S(1)} %copy-done.1), custom_call_target="tpu_custom_call" | custom-call | tf_op jit(solution)/shard_map/stats/pallas_call | solution.py:170
  59.5 0.0 copy-start.3
  59.5 5.7 %all-to-all-start.2 = ((bf16[128,4,128]{2,1,0:T(4,128)(2,1)}), bf16[128,4,128]{2,1,0:T(4,128)(2,1)S(1)}, u32[]{:S(2)}, u32[]{:S(2)}) async-start(bf16[128,4,128]{2,1,0:T(4,128)(2,1)} %bitcast.9), calls=%async_computation.2 | async-start | bytes 262144 | tf_op jit(solution)/shard_map/all_to_all | solution.py:176
  65.2 0.0 copy-done.3
  65.3 12.2 %all-to-all-done.2 = bf16[128,4,128]{2,1,0:T(4,128)(2,1)S(1)} async-done(((bf16[128,4,128]{2,1,0:T(4,128)(2,1)}), bf16[128,4,128]{2,1,0:T(4,128)(2,1)S(1)}, u32[]{:S(2)}, u32[]{:S(2)}) %all-to-all-start.2) | async-done | bytes 131104 | tf_op jit(solution)/shard_map/all_to_all | solution.py:176
  77.5 1.0 %smooth.1 = bf16[128,512]{1,0:T(8,128)(2,1)} custom-call(bf16[512,128]{1,0:T(8,128)(2,1)S(1)} %bitcast.15, f32[9,32,128]{2,1,0:T(8,128)S(1)} %bitcast.14), custom_call_target="tpu_custom_call" | custom-call | tf_op jit(solution)/shard_map/smooth/pallas_call | solution.py:178
  (2 shorter events, 0.0 us)
Async XLA Ops:
  1.7 9.7 %copy-start.2 = (bf16[1,16,8,512]{3,2,1,0:T(8,128)(2,1)S(1)}, bf16[1,16,8,512]{3,2,1,0:T(8,128)(2,1)}, u32[]{:S(2)}) copy-start(bf16[1,16,8,512]{3,2,1,0:T(8,128)(2,1)} %param.5) | copy-start | bytes 393220
  1.7 29.8 %all-to-all-start = ((bf16[16,9,4,512]{3,2,1,0:T(4,128)(2,1)}), bf16[16,9,4,512]{3,2,1,0:T(4,128)(2,1)S(1)}, u32[]{:S(2)}, u32[]{:S(2)}) async-start(bf16[16,9,4,512]{3,2,1,0:T(4,128)(2,1)} %broadcast_in_dim.8), calls=%async_computation | async-start | bytes 1179648 | tf_op jit(solution)/shard_map/all_to_all | solution.py:151
  11.4 10.6 %collective-permute-start = (bf16[128,512]{1,0:T(8,128)(2,1)S(1)}, bf16[128,512]{1,0:T(8,128)(2,1)S(1)}, u32[]{:S(2)}, u32[]{:S(2)}) collective-permute-start(bf16[128,512]{1,0:T(8,128)(2,1)S(1)} %bitcast.18), channel_id=1, source_target_pairs={{0,128},{128,256},{256,384},{384,0},{1,129},{129,257},{257,385},{3... | collective-permute-start | bytes 393224 | tf_op jit(solution)/shard_map/ppermute | solution.py:154
  14.6 8.0 %collective-permute-start.1 = (bf16[128,512]{1,0:T(8,128)(2,1)S(1)}, bf16[128,512]{1,0:T(8,128)(2,1)S(1)}, u32[]{:S(2)}, u32[]{:S(2)}) collective-permute-start(bf16[128,512]{1,0:T(8,128)(2,1)S(1)} %bitcast.19), channel_id=1, source_target_pairs={{0,256},{128,384},{256,0},{384,128},{1,257},{129,385},{257,1},{385... | collective-permute-start | bytes 393224 | tf_op jit(solution)/shard_map/ppermute | solution.py:154
  18.9 5.8 %collective-permute-start.2 = (bf16[128,512]{1,0:T(8,128)(2,1)S(1)}, bf16[128,512]{1,0:T(8,128)(2,1)S(1)}, u32[]{:S(2)}, u32[]{:S(2)}) collective-permute-start(bf16[128,512]{1,0:T(8,128)(2,1)S(1)} %bitcast.20), channel_id=1, source_target_pairs={{0,384},{128,0},{256,128},{384,256},{1,385},{129,1},{257,129},{385... | collective-permute-start | bytes 393224 | tf_op jit(solution)/shard_map/ppermute | solution.py:154
  24.8 6.0 %collective-permute-start.3 = (bf16[4,128,512]{2,1,0:T(8,128)(2,1)S(1)}, bf16[4,128,512]{2,1,0:T(8,128)(2,1)S(1)}, u32[]{:S(2)}, u32[]{:S(2)}) collective-permute-start(bf16[4,128,512]{2,1,0:T(8,128)(2,1)S(1)} %pad_maximum_fusion.own_ref), channel_id=1, source_target_pairs={{0,4},{4,0},{1,5},{5,1},{2,6},{6,2},{3,7},{7,3},{8,12},{12,8},{9,1... | collective-permute-start | bytes 1572872 | tf_op jit(solution)/shard_map/ppermute | solution.py:156
  31.5 25.1 %copy-start.1 = (bf16[128,128]{1,0:T(8,128)(2,1)S(1)}, bf16[128,128]{1,0:T(8,128)(2,1)}, u32[]{:S(2)}) copy-start(bf16[128,128]{1,0:T(8,128)(2,1)} %constant.5.clone.lanes_ref) | copy-start | bytes 98308
  32.8 23.9 %copy-start = (bf16[8,128,128]{2,1,0:T(8,128)(2,1)S(1)}, bf16[8,128,128]{2,1,0:T(8,128)(2,1)}, u32[]{:S(2)}) copy-start(bf16[8,128,128]{2,1,0:T(8,128)(2,1)} %constant.4.clone.pick_ref) | copy-start | bytes 786436
  59.5 5.7 %copy-start.3 = (f32[3,3,512]{2,1,0:T(4,128)S(1)}, f32[3,3,512]{2,1,0:T(4,128)}, u32[]{:S(2)}) copy-start(f32[3,3,512]{2,1,0:T(4,128)} %param.7) | copy-start | bytes 55300
  59.5 17.9 %all-to-all-start.2 = ((bf16[128,4,128]{2,1,0:T(4,128)(2,1)}), bf16[128,4,128]{2,1,0:T(4,128)(2,1)S(1)}, u32[]{:S(2)}, u32[]{:S(2)}) async-start(bf16[128,4,128]{2,1,0:T(4,128)(2,1)} %bitcast.9), calls=%async_computation.2 | async-start | bytes 262144 | tf_op jit(solution)/shard_map/all_to_all | solution.py:176

commit v2 on v1

--- a/solution.py
+++ b/solution.py
@@ -6,7 +6,7 @@
 from jax.experimental.pallas import tpu as pltpu
 from jax.sharding import Mesh, PartitionSpec as P
 
-ITERS = 2
+
 RIDGE = 0.5
 NX, NZ, NY, NC = 4, 2, 8, 2
 ROWS, COLS, CH, IMAGES = 16, 8, 512, 128
@@ -15,12 +15,11 @@
 NT = (((1,), (1,)), ((), ()))
 
 
-def vmem_call(body, out_shape, scratch, name):
+def vmem_call(body, out_shape, scratch):
     return pl.pallas_call(
         body,
         out_shape=out_shape,
         scratch_shapes=scratch,
-        name=name,
         compiler_params=pltpu.CompilerParams(vmem_limit_bytes=48 * 1024 * 1024),
     )
 
@@ -66,8 +65,16 @@
         out_ref[h * 32 : (h + 1) * 32, :] = packed.reshape(32, 128).astype(BF16)
 
 
-def exact_dot(a, b):
-    return jnp.dot(a, b, precision=lax.Precision.HIGHEST, preferred_element_type=F32)
+def split(a):
+    high = a.astype(BF16)
+    return high, (a - high.astype(F32)).astype(BF16)
+
+
+def fine_dot(a, b):
+    (ah, al), (bh, bl) = a, b
+    total = jnp.dot(ah, bl, preferred_element_type=F32)
+    total = total + jnp.dot(al, bh, preferred_element_type=F32)
+    return total + jnp.dot(ah, bh, preferred_element_type=F32)
 
 
 def stats_body(got_ref, pick_ref, lanes_ref, out_ref, rows_ref):
@@ -81,8 +88,8 @@
     gram = None
     for k in range(NX):
         block = got_ref[k * 128 : (k + 1) * 128, :]
-        from0 = jnp.dot(pick_ref[2 * k], block, preferred_element_type=F32)
-        from1 = jnp.dot(pick_ref[2 * k + 1], block, preferred_element_type=F32)
+        picked = jnp.dot(pick_ref[...], block, preferred_element_type=F32)
+        from0, from1 = picked[:IMAGES], picked[IMAGES:]
         same = jnp.where(lane_lo, from0, from1)
         swapped = pltpu.roll(jnp.where(lane_lo, from1, from0), 64, 1)
         mixed = jnp.where(even_row, same, swapped).astype(BF16)
@@ -93,19 +100,14 @@
         part = lax.dot_general(x, x, NT, preferred_element_type=F32)
         gram = part if gram is None else gram + part
     scaled = gram / (IMAGES - 1)
-    trace = jnp.sum(scaled * eye)
-    frob = jnp.sqrt(jnp.sum(scaled * scaled) + 2.0 * RIDGE * trace + RIDGE * RIDGE * CH)
-    upper = (scaled + RIDGE * eye) / frob
-    lower = 1.5 * eye - 0.5 * upper
-    upper = exact_dot(upper, lower)
-    for sweep in range(1, ITERS):
-        factor = 1.5 * eye - 0.5 * exact_dot(lower, upper)
-        if sweep + 1 < ITERS:
-            upper = exact_dot(upper, factor)
-        lower = exact_dot(factor, lower)
-    lower = lower / jnp.sqrt(frob)
-    high = lower.astype(BF16)
-    low = (lower - high.astype(F32)).astype(BF16)
+    squares = jnp.sum(scaled * (scaled + (2.0 * RIDGE) * eye))
+    frob = jnp.sqrt(squares + RIDGE * RIDGE * CH)
+    u = (scaled + RIDGE * eye) / frob
+    u_parts = split(u)
+    v = fine_dot(u_parts, u_parts)
+    high = fine_dot(split(v), split(0.0625 * v - 0.5625 * u))
+    lower = (2.25 * eye - 2.4375 * u) + 1.6875 * v + high
+    high, low = split(lower / jnp.sqrt(frob))
     for k in range(NX):
         white = jnp.dot(high, centered[k], preferred_element_type=F32)
         white = white + jnp.dot(low, centered[k], preferred_element_type=F32)
@@ -127,59 +129,52 @@
 
 
 def pick_tables():
-    picks = np.zeros((2 * NX, IMAGES, 128), np.float32)
-    for x in range(NX):
-        for c in range(NC):
-            for n in range(IMAGES):
-                xs, zy = n // 32, (n // 2) % 16
-                picks[2 * x + c, n, zy * 8 + c * 4 + (x - xs) % NX] = 1.0
+    picks = np.zeros((NC, IMAGES, 128), np.float32)
+    for c in range(NC):
+        for n in range(IMAGES):
+            xs, zy = n // 32, (n // 2) % 16
+            picks[c, n, zy * 8 + c * 4 + xs] = 1.0
     lanes = np.zeros((128, 128), np.float32)
     for c in range(NC):
         for zy in range(16):
             for k in range(4):
                 lanes[c * 64 + zy * 4 + k, zy * 8 + c * 4 + k] = 1.0
-    return picks, lanes
+    return picks.reshape(NC * IMAGES, 128), lanes
 
 
 PICKS, LANES = pick_tables()
 
 
+def exchange(value, axes):
+    return lax.all_to_all(value, axes, 0, 0, tiled=True)
+
+
 def shards(backbone, conv_weight, smooth_weight):
     image = backbone.reshape(ROWS * COLS, CH)
     chunk = conv_weight.transpose(0, 1, 3, 2).reshape(9, 4, CH)
-    spread = jnp.broadcast_to(chunk[None], (NZ * NY, 9, 4, CH))
-    kernels = lax.all_to_all(spread, ("z", "y"), 0, 0, tiled=True)
-    own = [image]
-    for k in range(1, NX):
-        own.append(lax.ppermute(image, "x", [(i, (i + k) % NX) for i in range(NX)]))
-    own = jnp.stack(own)
+    kernels = exchange(
+        jnp.broadcast_to(chunk[None], (NZ * NY,) + chunk.shape), ("z", "y")
+    )
+    own = lax.all_gather(image, "x")
     partner = lax.ppermute(own, "c", [(0, 1), (1, 0)])
     x = vmem_call(
-        interleave_body,
-        jax.ShapeDtypeStruct((1024, CH), BF16),
-        [pltpu.VMEM((4, 1024, 128), F32)],
-        "interleave",
+        interleave_body, jax.ShapeDtypeStruct((1024, CH), BF16), [pltpu.VMEM((4, 1024, 128), F32)]
     )(own, partner)
     features = vmem_call(
         conv_body,
         jax.ShapeDtypeStruct((512, 128), BF16),
         [pltpu.VMEM((640, CH), F32), pltpu.VMEM((18, 10, 8, 640), F32)],
-        "conv",
     )(kernels, x)
-    got = lax.all_to_all(features.reshape(128, 4, 128), AXES, 0, 0, tiled=True)
+    got = exchange(features.reshape(128, 4, 128), AXES)
     white = vmem_call(
-        stats_body,
-        jax.ShapeDtypeStruct((512, 128), BF16),
-        [pltpu.VMEM((512, 128), F32)],
-        "stats",
+        stats_body, jax.ShapeDtypeStruct((512, 128), BF16), [pltpu.VMEM((512, 128), F32)]
     )(got.reshape(512, 128), jnp.asarray(PICKS, BF16), jnp.asarray(LANES, BF16))
-    back = lax.all_to_all(white.reshape(128, 4, 128), AXES, 0, 0, tiled=True)
+    back = exchange(white.reshape(128, 4, 128), AXES)
     taps = jnp.tile(smooth_weight.reshape(9, 4, 128), (1, 8, 1))
     out = vmem_call(
         smooth_body,
         jax.ShapeDtypeStruct((128, CH), BF16),
         [pltpu.VMEM((18, 40, 128), F32), pltpu.VMEM((512, 128), F32)],
-        "smooth",
     )(back.reshape(512, 128), taps)
     return out.reshape(1, ROWS, COLS, CH)
 

time: 79 us -> 77.1 us (0.976)
  blocking collectives: 23.8 us -> 35.8 us
  starting transfers between devices: 30.4 us -> 19.7 us
  waiting for transfers between devices: 16.5 us -> 13.7 us
    all_gather x0 -> x1, blocking collectives: none -> 11.6 us  [shards(): own = lax.all_gather(image, 'x')]
    ppermute x3 -> x0, starting transfers between devices: 10.5 us -> none  [shards(): own.append(lax.ppermute(image, 'x', [(i, (i + k) % NX) for i in range(NX)]))]
    ppermute x3 -> x0, waiting for transfers between devices: 2.75 us -> none  [shards(): own.append(lax.ppermute(image, 'x', [(i, (i + k) % NX) for i in range(NX)]))]
  transfers between devices with their start and end apart: 6 -> 3, of which waited for: 4 -> 2; matrix products, arithmetic and copies ran while one was open for 0% -> 0% of each run, Pallas kernels for 1% -> 1%
where the time goes in v2:
time: 77.1 us; the launch traced here: 76.6 us
  blocking collectives  35.8 us (46%)
  starting transfers between devices  19.7 us (26%)
  waiting for transfers between devices  13.7 us (18%)
  Pallas kernels  5.52 us (7%)
  local copies, waits for them, and re-layouts  1.8 us (2%)
    all_to_all x1, blocking collectives, exchange(): return lax.all_to_all(value, axes, 0, 0, tiled=True)  24.2 us
    all_to_all x2, starting transfers between devices, exchange(): return lax.all_to_all(value, axes, 0, 0, tiled=True)  15.4 us
    all_to_all x2, waiting for transfers between devices, exchange(): return lax.all_to_all(value, axes, 0, 0, tiled=True)  12.2 us
    all_gather x1, blocking collectives, shards(): own = lax.all_gather(image, 'x')  11.6 us
    ppermute x1, starting transfers between devices, shards(): partner = lax.ppermute(own, 'c', [(0, 1), (1, 0)])  4.35 us
    pallas_call x1, Pallas kernels, shards(): vmem_call(stats_body, jax.ShapeDtypeStruct((512, 128), BF16), [pltpu.VMEM...  2.61 us
    broadcast_in_dim x1, local copies, waits for them, and re-layouts, shards(): jnp.broadcast_to(chunk[None], (NZ * NY,) + chunk.shape)  1.74 us
  transfers between devices with their start and end apart: 3, of which 2 were waited for; matrix products, arithmetic and copies ran while one was open for 0% of the time, Pallas kernels for 1%

profile of v2, /device:TPU:1, one launch (start us, length us, event | category | flops | bytes accessed | tf_op | source)
XLA Modules:
  0.0 76.6 jit_solution(4809453492730460265)
XLA Ops:
  0.0 1.7 %broadcast_in_dim.8 = bf16[16,9,4,512]{3,2,1,0:T(4,128)(2,1)} broadcast(bf16[9,4,512]{2,1,0:T(4,128)(2,1)} %bitcast.15), dimensions={1,2,3} | broadcast | bytes 626688 | tf_op jit(solution)/shard_map/broadcast_in_dim | solution.py:156
  1.7 0.0 copy-start.2
  1.7 9.7 %all-to-all-start = ((bf16[16,9,4,512]{3,2,1,0:T(4,128)(2,1)}), bf16[16,9,4,512]{3,2,1,0:T(4,128)(2,1)S(1)}, u32[]{:S(2)}, u32[]{:S(2)}) async-start(bf16[16,9,4,512]{3,2,1,0:T(4,128)(2,1)} %broadcast_in_dim.8), calls=%async_computation | async-start | bytes 1179648 | tf_op jit(solution)/shard_map/all_to_all | solution.py:149
  11.4 0.0 copy-done.2
  11.4 11.6 %all_gather.3.own_ref = bf16[4,128,512]{2,1,0:T(8,128)(2,1)S(1)} all-gather(bf16[1,128,512]{2,1,0:T(8,128)(2,1)S(1)} %bitcast.14), channel_id=1, replica_groups=mesh['x'=4,'z'=2,'y'=8,'c'=2,'rep'=4] {'x'}, dimensions={0}, use_global_device_ids=true | all-gather | bytes 655360 | tf_op jit(solution)/shard_map/all_gather | solution.py:158
  23.1 4.3 %collective-permute-start = (bf16[4,128,512]{2,1,0:T(8,128)(2,1)S(1)}, bf16[4,128,512]{2,1,0:T(8,128)(2,1)S(1)}, u32[]{:S(2)}, u32[]{:S(2)}) collective-permute-start(bf16[4,128,512]{2,1,0:T(8,128)(2,1)S(1)} %all_gather.3.own_ref), channel_id=1, source_target_pairs={{0,4},{4,0},{1,5},{5,1},{2,6},{6,2},{3,7},{7,3},{8,12},{12,8},{9,1... | collective-permute-start | bytes 1572872 | tf_op jit(solution)/shard_map/ppermute | solution.py:159
  27.4 1.5 %collective-permute-done.partner_ref = bf16[4,128,512]{2,1,0:T(8,128)(2,1)S(1)} collective-permute-done((bf16[4,128,512]{2,1,0:T(8,128)(2,1)S(1)}, bf16[4,128,512]{2,1,0:T(8,128)(2,1)S(1)}, u32[]{:S(2)}, u32[]{:S(2)}) %collective-permute-start) | collective-permute-done | bytes 524320 | tf_op jit(solution)/shard_map/ppermute | solution.py:159
  29.0 0.7 shard_map.55.x_ref
  29.6 0.0 all-to-all-done.weight_ref
  29.6 1.3 %shard_map.56 = bf16[512,128]{1,0:T(8,128)(2,1)S(1)} custom-call(bf16[16,9,4,512]{3,2,1,0:T(4,128)(2,1)S(1)} %all-to-all-done.weight_ref, bf16[1024,512]{1,0:T(8,128)(2,1)S(1)} %shard_map.55.x_ref), custom_call_target="tpu_custom_call" | custom-call | tf_op jit(solution)/shard_map/pallas_call | solution.py:163
  30.9 0.0 copy-start
  30.9 0.0 copy-start.1
  30.9 24.2 %all_to_all.15 = bf16[128,4,128]{2,1,0:T(4,128)(2,1)S(1)} all-to-all(bf16[128,4,128]{2,1,0:T(4,128)(2,1)S(1)} %bitcast.12), channel_id=1, replica_groups=mesh['x'=4,'z'=2,'y'=8,'c'=2,'rep'=4] {'x','z','y','c'}, dimensions={0} | all-to-all | bytes 262144 | tf_op jit(solution)/shard_map/all_to_all | solution.py:149
  55.1 0.0 copy-done
  55.1 0.0 copy-done.1
  55.1 2.6 %shard_map.57 = bf16[512,128]{1,0:T(8,128)(2,1)} custom-call(bf16[512,128]{1,0:T(8,128)(2,1)S(1)} %bitcast.13, bf16[256,128]{1,0:T(8,128)(2,1)S(1)} %copy-done, bf16[128,128]{1,0:T(8,128)(2,1)S(1)} %copy-done.1), custom_call_target="tpu_custom_call" | custom-call | tf_op jit(solution)/shard_map/pallas_call | solution.py:169
  57.7 0.0 copy-start.3
  57.7 5.7 %all-to-all-start.2 = ((bf16[128,4,128]{2,1,0:T(4,128)(2,1)}), bf16[128,4,128]{2,1,0:T(4,128)(2,1)S(1)}, u32[]{:S(2)}, u32[]{:S(2)}) async-start(bf16[128,4,128]{2,1,0:T(4,128)(2,1)} %bitcast.5), calls=%async_computation.2 | async-start | bytes 262144 | tf_op jit(solution)/shard_map/all_to_all | solution.py:149
  63.4 0.0 copy-done.3
  63.5 12.2 %all-to-all-done.2 = bf16[128,4,128]{2,1,0:T(4,128)(2,1)S(1)} async-done(((bf16[128,4,128]{2,1,0:T(4,128)(2,1)}), bf16[128,4,128]{2,1,0:T(4,128)(2,1)S(1)}, u32[]{:S(2)}, u32[]{:S(2)}) %all-to-all-start.2) | async-done | bytes 131104 | tf_op jit(solution)/shard_map/all_to_all | solution.py:149
  75.7 1.0 %shard_map.58 = bf16[128,512]{1,0:T(8,128)(2,1)} custom-call(bf16[512,128]{1,0:T(8,128)(2,1)S(1)} %bitcast.11, f32[9,32,128]{2,1,0:T(8,128)S(1)} %bitcast.10), custom_call_target="tpu_custom_call" | custom-call | tf_op jit(solution)/shard_map/pallas_call | solution.py:174
  (2 shorter events, 0.0 us)
Async XLA Ops:
  1.7 9.7 %copy-start.2 = (bf16[1,16,8,512]{3,2,1,0:T(8,128)(2,1)S(1)}, bf16[1,16,8,512]{3,2,1,0:T(8,128)(2,1)}, u32[]{:S(2)}) copy-start(bf16[1,16,8,512]{3,2,1,0:T(8,128)(2,1)} %param.5) | copy-start | bytes 393220
  1.7 27.9 %all-to-all-start = ((bf16[16,9,4,512]{3,2,1,0:T(4,128)(2,1)}), bf16[16,9,4,512]{3,2,1,0:T(4,128)(2,1)S(1)}, u32[]{:S(2)}, u32[]{:S(2)}) async-start(bf16[16,9,4,512]{3,2,1,0:T(4,128)(2,1)} %broadcast_in_dim.8), calls=%async_computation | async-start | bytes 1179648 | tf_op jit(solution)/shard_map/all_to_all | solution.py:149
  23.1 5.9 %collective-permute-start = (bf16[4,128,512]{2,1,0:T(8,128)(2,1)S(1)}, bf16[4,128,512]{2,1,0:T(8,128)(2,1)S(1)}, u32[]{:S(2)}, u32[]{:S(2)}) collective-permute-start(bf16[4,128,512]{2,1,0:T(8,128)(2,1)S(1)} %all_gather.3.own_ref), channel_id=1, source_target_pairs={{0,4},{4,0},{1,5},{5,1},{2,6},{6,2},{3,7},{7,3},{8,12},{12,8},{9,1... | collective-permute-start | bytes 1572872 | tf_op jit(solution)/shard_map/ppermute | solution.py:159
  30.9 24.2 %copy-start = (bf16[256,128]{1,0:T(8,128)(2,1)S(1)}, bf16[256,128]{1,0:T(8,128)(2,1)}, u32[]{:S(2)}) copy-start(bf16[256,128]{1,0:T(8,128)(2,1)} %constant.4.clone.pick_ref) | copy-start | bytes 196612
  30.9 24.2 %copy-start.1 = (bf16[128,128]{1,0:T(8,128)(2,1)S(1)}, bf16[128,128]{1,0:T(8,128)(2,1)}, u32[]{:S(2)}) copy-start(bf16[128,128]{1,0:T(8,128)(2,1)} %constant.5.clone.lanes_ref) | copy-start | bytes 98308
  57.7 5.7 %copy-start.3 = (f32[3,3,512]{2,1,0:T(4,128)S(1)}, f32[3,3,512]{2,1,0:T(4,128)}, u32[]{:S(2)}) copy-start(f32[3,3,512]{2,1,0:T(4,128)} %param.7) | copy-start | bytes 55300
  57.7 17.9 %all-to-all-start.2 = ((bf16[128,4,128]{2,1,0:T(4,128)(2,1)}), bf16[128,4,128]{2,1,0:T(4,128)(2,1)S(1)}, u32[]{:S(2)}, u32[]{:S(2)}) async-start(bf16[128,4,128]{2,1,0:T(4,128)(2,1)} %bitcast.5), calls=%async_computation.2 | async-start | bytes 262144 | tf_op jit(solution)/shard_map/all_to_all | solution.py:149

commit v3 on v2

--- a/solution.py
+++ b/solution.py
@@ -1,4 +1,3 @@
-import numpy as np
 import jax
 import jax.numpy as jnp
 from jax import lax
@@ -35,11 +34,11 @@
 
 def conv_body(weight_ref, x_ref, out_ref, wide_ref, z_ref):
     taps, group = weight_ref.shape[1], weight_ref.shape[0]
+    wide_ref[512:640, :] = jnp.zeros((128, CH), F32)
     for t in range(taps):
         for g in range(group):
-            at = t * 64 + g * 4
+            at = (t // 2) * 128 + g * 8 + (t % 2) * 4
             wide_ref[at : at + 4, :] = weight_ref[g, t].astype(F32)
-    wide_ref[576:640, :] = jnp.zeros((64, CH), F32)
     z_ref[0] = jnp.zeros((10, 8, 640), F32)
     z_ref[17] = jnp.zeros((10, 8, 640), F32)
     z_ref[:, 0] = jnp.zeros((18, 8, 640), F32)
@@ -48,7 +47,7 @@
     for lo, hi in ((0, 256), (256, 512), (512, 640)):
         part = lax.dot_general(x, wide_ref[lo:hi, :].astype(BF16), NT, preferred_element_type=F32)
         z_ref[1:17, 1:9, :, lo:hi] = part.reshape(ROWS, COLS, 8, hi - lo)
-    lane_lo = lax.broadcasted_iota(jnp.int32, (4, 8, 128), 2) < 64
+    slot0 = lax.broadcasted_iota(jnp.int32, (4, 8, 128), 2) % 8 < 4
     row_lo = lax.broadcasted_iota(jnp.int32, (4, 8, 128), 1) < 4
     for h in range(ROWS):
         sums = [None, None]
@@ -56,12 +55,12 @@
             a, b, tile = t // 3, t % 3, (t // 2) * 128
             piece = z_ref[h + a, b : b + 8, :, tile : tile + 128]
             sums[t % 2] = piece if sums[t % 2] is None else sums[t % 2] + piece
-        total = sums[0] + pltpu.roll(sums[1], 64, 2)
+        total = sums[0] + pltpu.roll(sums[1], 124, 2)
         pairs = total.reshape(4, 2, 8, 128)
         even, odd = pairs[:, 0], pairs[:, 1]
         first = jnp.where(row_lo, even, pltpu.roll(odd, 4, 1))
         second = jnp.where(row_lo, pltpu.roll(even, 4, 1), odd)
-        packed = jnp.where(lane_lo, first, pltpu.roll(second, 64, 2))
+        packed = jnp.where(slot0, first, pltpu.roll(second, 4, 2))
         out_ref[h * 32 : (h + 1) * 32, :] = packed.reshape(32, 128).astype(BF16)
 
 
@@ -77,9 +76,10 @@
     return total + jnp.dot(ah, bh, preferred_element_type=F32)
 
 
-def stats_body(got_ref, pick_ref, lanes_ref, out_ref, rows_ref):
-    lane_lo = lax.broadcasted_iota(jnp.int32, (IMAGES, 128), 1) < 64
-    even_row = lax.broadcasted_iota(jnp.int32, (IMAGES, 128), 0) % 2 == 0
+def stats_body(got_ref, out_ref, turn_ref, rows_ref):
+    tiles = (16, 8, 128)
+    slot0 = lax.broadcasted_iota(jnp.int32, tiles, 2) % 8 < 4
+    row_lo = lax.broadcasted_iota(jnp.int32, tiles, 1) < 4
     eye = (
         lax.broadcasted_iota(jnp.int32, (IMAGES, IMAGES), 0)
         == lax.broadcasted_iota(jnp.int32, (IMAGES, IMAGES), 1)
@@ -87,31 +87,32 @@
     centered = []
     gram = None
     for k in range(NX):
-        block = got_ref[k * 128 : (k + 1) * 128, :]
-        picked = jnp.dot(pick_ref[...], block, preferred_element_type=F32)
-        from0, from1 = picked[:IMAGES], picked[IMAGES:]
-        same = jnp.where(lane_lo, from0, from1)
-        swapped = pltpu.roll(jnp.where(lane_lo, from1, from0), 64, 1)
-        mixed = jnp.where(even_row, same, swapped).astype(BF16)
-        x = jnp.dot(mixed, lanes_ref[...], preferred_element_type=F32)
+        v = got_ref[k * 128 : (k + 1) * 128, :].astype(F32).reshape(tiles)
+        mixed = jnp.where(slot0, v, pltpu.roll(v, 4, 1))
+        turned = jnp.where(slot0, pltpu.roll(mixed, 124, 2), pltpu.roll(mixed, 4, 2))
+        x = jnp.where(row_lo, mixed, turned).reshape(IMAGES, 128)
         center = jnp.sum(x, axis=0, keepdims=True) / IMAGES
         x = (x - center).astype(BF16)
         centered.append(x)
         part = lax.dot_general(x, x, NT, preferred_element_type=F32)
         gram = part if gram is None else gram + part
     scaled = gram / (IMAGES - 1)
+    ridged = scaled + RIDGE * eye
+    parts = split(ridged)
+    square = fine_dot(parts, parts)
     squares = jnp.sum(scaled * (scaled + (2.0 * RIDGE) * eye))
     frob = jnp.sqrt(squares + RIDGE * RIDGE * CH)
-    u = (scaled + RIDGE * eye) / frob
-    u_parts = split(u)
-    v = fine_dot(u_parts, u_parts)
+    inverse = 1.0 / frob
+    u = ridged * inverse
+    v = square * inverse * inverse
     high = fine_dot(split(v), split(0.0625 * v - 0.5625 * u))
     lower = (2.25 * eye - 2.4375 * u) + 1.6875 * v + high
     high, low = split(lower / jnp.sqrt(frob))
     for k in range(NX):
         white = jnp.dot(high, centered[k], preferred_element_type=F32)
-        white = white + jnp.dot(low, centered[k], preferred_element_type=F32)
-        rows_ref[pl.ds(k, IMAGES, stride=4), :] = white
+        turn_ref[k] = white + jnp.dot(low, centered[k], preferred_element_type=F32)
+        for xs in range(NX):
+            rows_ref[pl.ds(xs * 128 + k, 32, stride=4), :] = turn_ref[k, pl.ds(xs, 32, stride=4), :]
     out_ref[...] = rows_ref[...].astype(BF16)
 
 
@@ -126,23 +127,6 @@
     rows_ref[...] = total.reshape(512, 128)
     for k in range(NX):
         out_ref[:, k * 128 : (k + 1) * 128] = rows_ref[pl.ds(k, 128, stride=4), :].astype(BF16)
-
-
-def pick_tables():
-    picks = np.zeros((NC, IMAGES, 128), np.float32)
-    for c in range(NC):
-        for n in range(IMAGES):
-            xs, zy = n // 32, (n // 2) % 16
-            picks[c, n, zy * 8 + c * 4 + xs] = 1.0
-    lanes = np.zeros((128, 128), np.float32)
-    for c in range(NC):
-        for zy in range(16):
-            for k in range(4):
-                lanes[c * 64 + zy * 4 + k, zy * 8 + c * 4 + k] = 1.0
-    return picks.reshape(NC * IMAGES, 128), lanes
-
-
-PICKS, LANES = pick_tables()
 
 
 def exchange(value, axes):
@@ -165,12 +149,15 @@
         jax.ShapeDtypeStruct((512, 128), BF16),
         [pltpu.VMEM((640, CH), F32), pltpu.VMEM((18, 10, 8, 640), F32)],
     )(kernels, x)
+    taps = jnp.tile(smooth_weight.reshape(9, 4, 128), (1, 8, 1))
+    features, taps = lax.optimization_barrier((features, taps))
     got = exchange(features.reshape(128, 4, 128), AXES)
     white = vmem_call(
-        stats_body, jax.ShapeDtypeStruct((512, 128), BF16), [pltpu.VMEM((512, 128), F32)]
-    )(got.reshape(512, 128), jnp.asarray(PICKS, BF16), jnp.asarray(LANES, BF16))
+        stats_body,
+        jax.ShapeDtypeStruct((512, 128), BF16),
+        [pltpu.VMEM((NX, 128, 128), F32), pltpu.VMEM((512, 128), F32)],
+    )(got.reshape(512, 128))
     back = exchange(white.reshape(128, 4, 128), AXES)
-    taps = jnp.tile(smooth_weight.reshape(9, 4, 128), (1, 8, 1))
     out = vmem_call(
         smooth_body,
         jax.ShapeDtypeStruct((128, CH), BF16),

time: 77.1 us -> 74.5 us (0.966)
  blocking collectives: 35.8 us -> 52.8 us
  waiting for transfers between devices: 13.7 us -> 1.48 us
  starting transfers between devices: 19.7 us -> 14 us
  Pallas kernels: 5.52 us -> 3.93 us
    all_to_all x1 -> x2, blocking collectives: 24.2 us -> 41.2 us  [exchange(): return lax.all_to_all(value, axes, 0, 0, tiled=True)]
    all_to_all x2 -> x1, waiting for transfers between devices: 12.2 us -> 0.01 us  [exchange(): return lax.all_to_all(value, axes, 0, 0, tiled=True)]
    all_to_all x2 -> x1, starting transfers between devices: 15.4 us -> 9.68 us  [exchange(): return lax.all_to_all(value, axes, 0, 0, tiled=True)]
    pallas_call x1, Pallas kernels: 2.61 us -> 1 us  [shards(): vmem_call(stats_body, jax.ShapeDtypeStruct((512, 128), BF16), [pltpu.VMEM...]
  transfers between devices with their start and end apart: 3 -> 2, of which waited for: 2 -> 1; matrix products, arithmetic and copies ran while one was open for 0% -> 0% of each run, Pallas kernels for 1% -> 1%
where the time goes in v3:
time: 74.5 us; the launch traced here: 74.1 us
  blocking collectives  52.8 us (71%)
  starting transfers between devices  14 us (19%)
  Pallas kernels  3.93 us (5%)
  local copies, waits for them, and re-layouts  1.8 us (2%)
  waiting for transfers between devices  1.48 us (2%)
    all_to_all x2, blocking collectives, exchange(): return lax.all_to_all(value, axes, 0, 0, tiled=True)  41.2 us
    all_gather x1, blocking collectives, shards(): own = lax.all_gather(image, 'x')  11.6 us
    all_to_all x1, starting transfers between devices, exchange(): return lax.all_to_all(value, axes, 0, 0, tiled=True)  9.68 us
    ppermute x1, starting transfers between devices, shards(): partner = lax.ppermute(own, 'c', [(0, 1), (1, 0)])  4.35 us
    broadcast_in_dim x1, local copies, waits for them, and re-layouts, shards(): jnp.broadcast_to(chunk[None], (NZ * NY,) + chunk.shape)  1.75 us
  transfers between devices with their start and end apart: 2, of which 1 were waited for; matrix products, arithmetic and copies ran while one was open for 0% of the time, Pallas kernels for 1%

profile of v3, /device:TPU:1, one launch (start us, length us, event | category | flops | bytes accessed | tf_op | source)
XLA Modules:
  0.0 74.1 jit_solution(16813507985270935741)
XLA Ops:
  0.0 1.7 %broadcast_in_dim.8 = bf16[16,9,4,512]{3,2,1,0:T(4,128)(2,1)} broadcast(bf16[9,4,512]{2,1,0:T(4,128)(2,1)} %bitcast.16), dimensions={1,2,3} | broadcast | bytes 626688 | tf_op jit(solution)/shard_map/broadcast_in_dim | solution.py:140
  1.8 0.0 copy-start
  1.8 9.7 %all-to-all-start = ((bf16[16,9,4,512]{3,2,1,0:T(4,128)(2,1)}), bf16[16,9,4,512]{3,2,1,0:T(4,128)(2,1)S(1)}, u32[]{:S(2)}, u32[]{:S(2)}) async-start(bf16[16,9,4,512]{3,2,1,0:T(4,128)(2,1)} %broadcast_in_dim.8), calls=%async_computation | async-start | bytes 1179648 | tf_op jit(solution)/shard_map/all_to_all | solution.py:133
  11.4 0.0 copy-done
  11.5 0.0 copy-start.1
  11.5 11.6 %all_gather.3.own_ref = bf16[4,128,512]{2,1,0:T(8,128)(2,1)S(1)} all-gather(bf16[1,128,512]{2,1,0:T(8,128)(2,1)S(1)} %bitcast.15), channel_id=1, replica_groups=mesh['x'=4,'z'=2,'y'=8,'c'=2,'rep'=4] {'x'}, dimensions={0}, use_global_device_ids=true | all-gather | bytes 655360 | tf_op jit(solution)/shard_map/all_gather | solution.py:142
  23.1 4.3 %collective-permute-start = (bf16[4,128,512]{2,1,0:T(8,128)(2,1)S(1)}, bf16[4,128,512]{2,1,0:T(8,128)(2,1)S(1)}, u32[]{:S(2)}, u32[]{:S(2)}) collective-permute-start(bf16[4,128,512]{2,1,0:T(8,128)(2,1)S(1)} %all_gather.3.own_ref), channel_id=1, source_target_pairs={{0,4},{4,0},{1,5},{5,1},{2,6},{6,2},{3,7},{7,3},{8,12},{12,8},{9,1... | collective-permute-start | bytes 1572872 | tf_op jit(solution)/shard_map/ppermute | solution.py:143
  27.5 0.0 copy-done.1
  27.5 1.5 %collective-permute-done.partner_ref = bf16[4,128,512]{2,1,0:T(8,128)(2,1)S(1)} collective-permute-done((bf16[4,128,512]{2,1,0:T(8,128)(2,1)S(1)}, bf16[4,128,512]{2,1,0:T(8,128)(2,1)S(1)}, u32[]{:S(2)}, u32[]{:S(2)}) %collective-permute-start) | collective-permute-done | bytes 524320 | tf_op jit(solution)/shard_map/ppermute | solution.py:143
  29.0 0.7 shard_map.37.x_ref
  29.7 0.0 all-to-all-done.weight_ref
  29.7 1.3 %shard_map.38 = bf16[512,128]{1,0:T(8,128)(2,1)S(1)} custom-call(bf16[16,9,4,512]{3,2,1,0:T(4,128)(2,1)S(1)} %all-to-all-done.weight_ref, bf16[1024,512]{1,0:T(8,128)(2,1)S(1)} %shard_map.37.x_ref), custom_call_target="tpu_custom_call" | custom-call | tf_op jit(solution)/shard_map/pallas_call | solution.py:147
  31.0 24.0 %all_to_all.15 = bf16[128,4,128]{2,1,0:T(4,128)(2,1)S(1)} all-to-all(bf16[128,4,128]{2,1,0:T(4,128)(2,1)S(1)} %bitcast.11), channel_id=1, replica_groups=mesh['x'=4,'z'=2,'y'=8,'c'=2,'rep'=4] {'x','z','y','c'}, dimensions={0} | all-to-all | bytes 262144 | tf_op jit(solution)/shard_map/all_to_all | solution.py:133
  55.0 1.0 %shard_map.39 = bf16[512,128]{1,0:T(8,128)(2,1)S(1)} custom-call(bf16[512,128]{1,0:T(8,128)(2,1)S(1)} %bitcast.13), custom_call_target="tpu_custom_call" | custom-call | tf_op jit(solution)/shard_map/pallas_call | solution.py:155
  56.0 17.1 %all_to_all.16 = bf16[128,4,128]{2,1,0:T(4,128)(2,1)S(1)} all-to-all(bf16[128,4,128]{2,1,0:T(4,128)(2,1)S(1)} %bitcast.14), channel_id=1, replica_groups=mesh['x'=4,'z'=2,'y'=8,'c'=2,'rep'=4] {'x','z','y','c'}, dimensions={0} | all-to-all | bytes 262144 | tf_op jit(solution)/shard_map/all_to_all | solution.py:133
  73.1 1.0 %shard_map.40 = bf16[128,512]{1,0:T(8,128)(2,1)} custom-call(bf16[512,128]{1,0:T(8,128)(2,1)S(1)} %bitcast.12, f32[9,32,128]{2,1,0:T(8,128)S(1)} %bitcast.10), custom_call_target="tpu_custom_call" | custom-call | tf_op jit(solution)/shard_map/pallas_call | solution.py:161
  (2 shorter events, 0.0 us)
Async XLA Ops:
  1.8 9.7 %copy-start = (bf16[1,16,8,512]{3,2,1,0:T(8,128)(2,1)S(1)}, bf16[1,16,8,512]{3,2,1,0:T(8,128)(2,1)}, u32[]{:S(2)}) copy-start(bf16[1,16,8,512]{3,2,1,0:T(8,128)(2,1)} %param.3) | copy-start | bytes 393220
  1.8 27.9 %all-to-all-start = ((bf16[16,9,4,512]{3,2,1,0:T(4,128)(2,1)}), bf16[16,9,4,512]{3,2,1,0:T(4,128)(2,1)S(1)}, u32[]{:S(2)}, u32[]{:S(2)}) async-start(bf16[16,9,4,512]{3,2,1,0:T(4,128)(2,1)} %broadcast_in_dim.8), calls=%async_computation | async-start | bytes 1179648 | tf_op jit(solution)/shard_map/all_to_all | solution.py:133
  11.5 16.0 %copy-start.1 = (f32[3,3,512]{2,1,0:T(4,128)S(1)}, f32[3,3,512]{2,1,0:T(4,128)}, u32[]{:S(2)}) copy-start(f32[3,3,512]{2,1,0:T(4,128)} %param.5) | copy-start | bytes 55300
  23.1 5.9 %collective-permute-start = (bf16[4,128,512]{2,1,0:T(8,128)(2,1)S(1)}, bf16[4,128,512]{2,1,0:T(8,128)(2,1)S(1)}, u32[]{:S(2)}, u32[]{:S(2)}) collective-permute-start(bf16[4,128,512]{2,1,0:T(8,128)(2,1)S(1)} %all_gather.3.own_ref), channel_id=1, source_target_pairs={{0,4},{4,0},{1,5},{5,1},{2,6},{6,2},{3,7},{7,3},{8,12},{12,8},{9,1... | collective-permute-start | bytes 1572872 | tf_op jit(solution)/shard_map/ppermute | solution.py:143

commit v4 on v3

--- a/solution.py
+++ b/solution.py
@@ -23,45 +23,63 @@
     )
 
 
-def interleave_body(own_ref, partner_ref, out_ref, rows_ref):
+def spread_body(chunk_ref, out_ref, sems):
+    copies = [
+        pltpu.make_async_copy(chunk_ref, out_ref.at[g], sems.at[g]) for g in range(NZ * NY)
+    ]
+    for copy in copies:
+        copy.start()
+    for copy in copies:
+        copy.wait()
+
+
+def convolve(image_ref, wide, rows_ref, z_ref, put):
     for t in range(4):
-        lanes = slice(t * 128, (t + 1) * 128)
-        for j in range(4):
-            rows_ref[t, pl.ds(j, IMAGES, stride=8), :] = own_ref[j, :, lanes].astype(F32)
-            rows_ref[t, pl.ds(4 + j, IMAGES, stride=8), :] = partner_ref[j, :, lanes].astype(F32)
-        out_ref[:, lanes] = rows_ref[t].astype(BF16)
-
-
-def conv_body(weight_ref, x_ref, out_ref, wide_ref, z_ref):
-    taps, group = weight_ref.shape[1], weight_ref.shape[0]
-    wide_ref[512:640, :] = jnp.zeros((128, CH), F32)
-    for t in range(taps):
-        for g in range(group):
-            at = (t // 2) * 128 + g * 8 + (t % 2) * 4
-            wide_ref[at : at + 4, :] = weight_ref[g, t].astype(F32)
-    z_ref[0] = jnp.zeros((10, 8, 640), F32)
-    z_ref[17] = jnp.zeros((10, 8, 640), F32)
-    z_ref[:, 0] = jnp.zeros((18, 8, 640), F32)
-    z_ref[:, 9] = jnp.zeros((18, 8, 640), F32)
-    x = x_ref[...]
+        for j in range(NX):
+            rows_ref[t, pl.ds(j, IMAGES, stride=4), :] = image_ref[
+                j, :, t * 128 : (t + 1) * 128
+            ].astype(F32)
+    x = jnp.concatenate([rows_ref[t].astype(BF16) for t in range(4)], axis=1)
+    z_ref[:, 0] = jnp.zeros((5, 48, 128), F32)
+    z_ref[:, 17] = jnp.zeros((5, 48, 128), F32)
+    z_ref[:, :, 0:8] = jnp.zeros((5, 18, 8, 128), F32)
+    z_ref[:, :, 40:48] = jnp.zeros((5, 18, 8, 128), F32)
     for lo, hi in ((0, 256), (256, 512), (512, 640)):
-        part = lax.dot_general(x, wide_ref[lo:hi, :].astype(BF16), NT, preferred_element_type=F32)
-        z_ref[1:17, 1:9, :, lo:hi] = part.reshape(ROWS, COLS, 8, hi - lo)
-    slot0 = lax.broadcasted_iota(jnp.int32, (4, 8, 128), 2) % 8 < 4
-    row_lo = lax.broadcasted_iota(jnp.int32, (4, 8, 128), 1) < 4
+        part = lax.dot_general(x, wide(lo, hi), NT, preferred_element_type=F32)
+        for at in range(lo, hi, 128):
+            z_ref[at // 128, 1:17, 8:40] = part[:, at - lo : at - lo + 128].reshape(ROWS, 32, 128)
     for h in range(ROWS):
         sums = [None, None]
-        for t in range(taps):
-            a, b, tile = t // 3, t % 3, (t // 2) * 128
-            piece = z_ref[h + a, b : b + 8, :, tile : tile + 128]
+        for t in range(9):
+            a, b = t // 3, t % 3
+            piece = z_ref[t // 2, h + a, 4 + 4 * b : 36 + 4 * b, :]
             sums[t % 2] = piece if sums[t % 2] is None else sums[t % 2] + piece
-        total = sums[0] + pltpu.roll(sums[1], 124, 2)
-        pairs = total.reshape(4, 2, 8, 128)
-        even, odd = pairs[:, 0], pairs[:, 1]
-        first = jnp.where(row_lo, even, pltpu.roll(odd, 4, 1))
-        second = jnp.where(row_lo, pltpu.roll(even, 4, 1), odd)
-        packed = jnp.where(slot0, first, pltpu.roll(second, 4, 2))
-        out_ref[h * 32 : (h + 1) * 32, :] = packed.reshape(32, 128).astype(BF16)
+        put(h, sums[0] + pltpu.roll(sums[1], 124, 1))
+
+
+def conv_own_body(weight_ref, image_ref, out_ref, wide_ref, tall_ref, rows_ref, z_ref):
+    tall_ref[512:640, :] = jnp.zeros((128, CH), F32)
+    for t in range(9):
+        for g in range(NZ * NY):
+            at = (t // 2) * 128 + g * 8 + (t % 2) * 4
+            tall_ref[at : at + 4, :] = weight_ref[g, t].astype(F32)
+    wide_ref[...] = tall_ref[...].astype(BF16)
+
+    def put(h, total):
+        out_ref[h * 32 : (h + 1) * 32, :] = total.astype(BF16)
+
+    convolve(image_ref, lambda lo, hi: wide_ref[lo:hi, :], rows_ref, z_ref, put)
+
+
+def conv_partner_body(wide_ref, image_ref, own_ref, out_ref, rows_ref, z_ref):
+    slot0 = lax.broadcasted_iota(jnp.int32, (32, 128), 1) % 8 < 4
+
+    def put(h, total):
+        own = own_ref[h * 32 : (h + 1) * 32, :].astype(F32)
+        merged = jnp.where(slot0, own, pltpu.roll(total, 4, 1))
+        out_ref[h * 32 : (h + 1) * 32, :] = merged.astype(BF16)
+
+    convolve(image_ref, lambda lo, hi: wide_ref[lo:hi, :], rows_ref, z_ref, put)
 
 
 def split(a):
@@ -117,14 +135,18 @@
 
 
 def smooth_body(white_ref, weight_ref, out_ref, pad_ref, rows_ref):
-    pad_ref[...] = jnp.zeros((18, 40, 128), F32)
-    pad_ref[1:17, 4:36, :] = white_ref[...].astype(F32).reshape(ROWS, 32, 128)
-    total = None
-    for t in range(9):
-        a, b = t // 3, t % 3
-        piece = pad_ref[a : a + ROWS, 4 * b : 4 * b + 32, :] * weight_ref[t][None]
-        total = piece if total is None else total + piece
-    rows_ref[...] = total.reshape(512, 128)
+    pad_ref[0] = jnp.zeros((48, 128), F32)
+    pad_ref[17] = jnp.zeros((48, 128), F32)
+    pad_ref[:, 0:8] = jnp.zeros((18, 8, 128), F32)
+    pad_ref[:, 40:48] = jnp.zeros((18, 8, 128), F32)
+    pad_ref[1:17, 8:40, :] = white_ref[...].astype(F32).reshape(ROWS, 32, 128)
+    for h in range(ROWS):
+        total = None
+        for t in range(9):
+            a, b = t // 3, t % 3
+            piece = pad_ref[h + a, 4 + 4 * b : 36 + 4 * b, :].reshape(4, 8, 128) * weight_ref[t]
+            total = piece if total is None else total + piece
+        rows_ref[h * 32 : (h + 1) * 32, :] = total.reshape(32, 128)
     for k in range(NX):
         out_ref[:, k * 128 : (k + 1) * 128] = rows_ref[pl.ds(k, 128, stride=4), :].astype(BF16)
 
@@ -136,20 +158,26 @@
 def shards(backbone, conv_weight, smooth_weight):
     image = backbone.reshape(ROWS * COLS, CH)
     chunk = conv_weight.transpose(0, 1, 3, 2).reshape(9, 4, CH)
-    kernels = exchange(
-        jnp.broadcast_to(chunk[None], (NZ * NY,) + chunk.shape), ("z", "y")
-    )
+    spread = pl.pallas_call(
+        spread_body,
+        out_shape=jax.ShapeDtypeStruct((NZ * NY,) + chunk.shape, BF16),
+        in_specs=[pl.BlockSpec(memory_space=pl.ANY)],
+        out_specs=pl.BlockSpec(memory_space=pl.ANY),
+        scratch_shapes=[pltpu.SemaphoreType.DMA((NZ * NY,))],
+        name="spread",
+    )(chunk)
+    kernels = exchange(spread, ("z", "y"))
     own = lax.all_gather(image, "x")
     partner = lax.ppermute(own, "c", [(0, 1), (1, 0)])
-    x = vmem_call(
-        interleave_body, jax.ShapeDtypeStruct((1024, CH), BF16), [pltpu.VMEM((4, 1024, 128), F32)]
-    )(own, partner)
-    features = vmem_call(
-        conv_body,
-        jax.ShapeDtypeStruct((512, 128), BF16),
-        [pltpu.VMEM((640, CH), F32), pltpu.VMEM((18, 10, 8, 640), F32)],
-    )(kernels, x)
-    taps = jnp.tile(smooth_weight.reshape(9, 4, 128), (1, 8, 1))
+    rows = [pltpu.VMEM((4, 512, 128), F32), pltpu.VMEM((5, 18, 48, 128), F32)]
+    half = jax.ShapeDtypeStruct((512, 128), BF16)
+    first, wide = vmem_call(
+        conv_own_body,
+        (half, jax.ShapeDtypeStruct((640, CH), BF16)),
+        [pltpu.VMEM((640, CH), F32)] + rows,
+    )(kernels, own)
+    features = vmem_call(conv_partner_body, half, rows)(wide, partner, first)
+    taps = jnp.tile(smooth_weight.reshape(9, 4, 128), (1, 2, 1))
     features, taps = lax.optimization_barrier((features, taps))
     got = exchange(features.reshape(128, 4, 128), AXES)
     white = vmem_call(
@@ -161,7 +189,7 @@
     out = vmem_call(
         smooth_body,
         jax.ShapeDtypeStruct((128, CH), BF16),
-        [pltpu.VMEM((18, 40, 128), F32), pltpu.VMEM((512, 128), F32)],
+        [pltpu.VMEM((18, 48, 128), F32), pltpu.VMEM((512, 128), F32)],
     )(back.reshape(512, 128), taps)
     return out.reshape(1, ROWS, COLS, CH)
 

time: 74.5 us -> 90.6 us (1.22)
  Pallas kernels: 3.93 us -> 22.8 us
  local copies, waits for them, and re-layouts: 1.8 us -> 0.04 us
  waiting for transfers between devices: 1.48 us -> 0.5 us
    pallas_call x2 -> x3, Pallas kernels: 1.94 us -> 20.9 us  [the longest x1 19.1 us: shards(): pl.pallas_call(spread_body, out_shape=jax.ShapeDtypeStruct((NZ * NY,) + c...]
    broadcast_in_dim x1 -> x0, local copies, waits for them, and re-layouts: 1.75 us -> none  [shards(): jnp.broadcast_to(chunk[None], (NZ * NY,) + chunk.shape)]
    ppermute x1, waiting for transfers between devices: 1.48 us -> 0.49 us  [shards(): partner = lax.ppermute(own, 'c', [(0, 1), (1, 0)])]
where the time goes in v4:
time: 90.6 us; the launch traced here: 90.3 us
  blocking collectives  52.8 us (58%)
  Pallas kernels  22.8 us (25%)
  starting transfers between devices  14 us (15%)
    all_to_all x2, blocking collectives, exchange(): return lax.all_to_all(value, axes, 0, 0, tiled=True)  41.2 us
    pallas_call x1, Pallas kernels, shards(): pl.pallas_call(spread_body, out_shape=jax.ShapeDtypeStruct((NZ * NY,) + c...  19.1 us
    all_gather x1, blocking collectives, shards(): own = lax.all_gather(image, 'x')  11.6 us
    all_to_all x1, starting transfers between devices, exchange(): return lax.all_to_all(value, axes, 0, 0, tiled=True)  9.7 us
    ppermute x1, starting transfers between devices, shards(): partner = lax.ppermute(own, 'c', [(0, 1), (1, 0)])  4.35 us
  transfers between devices with their start and end apart: 2, of which 1 were waited for; matrix products, arithmetic and copies ran while one was open for 0% of the time, Pallas kernels for 1%

profile of v4, /device:TPU:1, one launch (start us, length us, event | category | flops | bytes accessed | tf_op | source)
XLA Modules:
  0.0 90.3 jit_solution(2382133934681182866)
XLA Ops:
  0.0 19.1 %spread.1 = bf16[16,9,4,512]{3,2,1,0:T(4,128)(2,1)} custom-call(bf16[9,4,512]{2,1,0:T(4,128)(2,1)} %bitcast.16), custom_call_target="tpu_custom_call" | custom-call | tf_op jit(solution)/shard_map/spread/pallas_call | solution.py:161
  19.1 0.0 copy-start
  19.1 9.7 %all-to-all-start = ((bf16[16,9,4,512]{3,2,1,0:T(4,128)(2,1)}), bf16[16,9,4,512]{3,2,1,0:T(4,128)(2,1)S(1)}, u32[]{:S(2)}, u32[]{:S(2)}) async-start(bf16[16,9,4,512]{3,2,1,0:T(4,128)(2,1)} %spread.1), calls=%async_computation | async-start | bytes 1179648 | tf_op jit(solution)/shard_map/all_to_all | solution.py:155
  28.8 0.0 copy-done
  28.8 0.0 copy-start.1
  28.9 11.6 %all_gather.3.image_ref = bf16[4,128,512]{2,1,0:T(8,128)(2,1)S(1)} all-gather(bf16[1,128,512]{2,1,0:T(8,128)(2,1)S(1)} %bitcast.15), channel_id=1, replica_groups=mesh['x'=4,'z'=2,'y'=8,'c'=2,'rep'=4] {'x'}, dimensions={0}, use_global_device_ids=true | all-gather | bytes 655360 | tf_op jit(solution)/shard_map/all_gather | solution.py:170
  40.5 4.3 %collective-permute-start = (bf16[4,128,512]{2,1,0:T(8,128)(2,1)S(1)}, bf16[4,128,512]{2,1,0:T(8,128)(2,1)S(1)}, u32[]{:S(2)}, u32[]{:S(2)}) collective-permute-start(bf16[4,128,512]{2,1,0:T(8,128)(2,1)S(1)} %all_gather.3.image_ref), channel_id=1, source_target_pairs={{0,4},{4,0},{1,5},{5,1},{2,6},{6,2},{3,7},{7,3},{8,12},{12,8},{9,1... | collective-permute-start | bytes 1572872 | tf_op jit(solution)/shard_map/ppermute | solution.py:171
  44.9 0.0 copy-done.1
  44.9 0.0 all-to-all-done.weight_ref
  44.9 1.0 %shard_map.37 = (bf16[512,128]{1,0:T(8,128)(2,1)S(1)}, bf16[640,512]{1,0:T(8,128)(2,1)S(1)}) custom-call(bf16[16,9,4,512]{3,2,1,0:T(4,128)(2,1)S(1)} %all-to-all-done.weight_ref, bf16[4,128,512]{2,1,0:T(8,128)(2,1)S(1)} %all_gather.3.image_ref), custom_call_target="tpu_custom_call" | custom-call | tf_op jit(solution)/shard_map/pallas_call | solution.py:174
  45.9 0.5 collective-permute-done.image_ref
  46.4 0.9 shard_map.38
  47.2 24.0 %all_to_all.15 = bf16[128,4,128]{2,1,0:T(4,128)(2,1)S(1)} all-to-all(bf16[128,4,128]{2,1,0:T(4,128)(2,1)S(1)} %bitcast.13), channel_id=1, replica_groups=mesh['x'=4,'z'=2,'y'=8,'c'=2,'rep'=4] {'x','z','y','c'}, dimensions={0} | all-to-all | bytes 262144 | tf_op jit(solution)/shard_map/all_to_all | solution.py:155
  71.3 1.0 %shard_map.39 = bf16[512,128]{1,0:T(8,128)(2,1)S(1)} custom-call(bf16[512,128]{1,0:T(8,128)(2,1)S(1)} %bitcast.11), custom_call_target="tpu_custom_call" | custom-call | tf_op jit(solution)/shard_map/pallas_call | solution.py:183
  72.3 17.1 %all_to_all.16 = bf16[128,4,128]{2,1,0:T(4,128)(2,1)S(1)} all-to-all(bf16[128,4,128]{2,1,0:T(4,128)(2,1)S(1)} %bitcast.12), channel_id=1, replica_groups=mesh['x'=4,'z'=2,'y'=8,'c'=2,'rep'=4] {'x','z','y','c'}, dimensions={0} | all-to-all | bytes 262144 | tf_op jit(solution)/shard_map/all_to_all | solution.py:155
  89.4 0.8 shard_map.40
  (2 shorter events, 0.0 us)
Async XLA Ops:
  19.1 9.7 %copy-start = (bf16[1,16,8,512]{3,2,1,0:T(8,128)(2,1)S(1)}, bf16[1,16,8,512]{3,2,1,0:T(8,128)(2,1)}, u32[]{:S(2)}) copy-start(bf16[1,16,8,512]{3,2,1,0:T(8,128)(2,1)} %param.3) | copy-start | bytes 393220
  19.1 25.8 %all-to-all-start = ((bf16[16,9,4,512]{3,2,1,0:T(4,128)(2,1)}), bf16[16,9,4,512]{3,2,1,0:T(4,128)(2,1)S(1)}, u32[]{:S(2)}, u32[]{:S(2)}) async-start(bf16[16,9,4,512]{3,2,1,0:T(4,128)(2,1)} %spread.1), calls=%async_computation | async-start | bytes 1179648 | tf_op jit(solution)/shard_map/all_to_all | solution.py:155
  28.8 16.0 %copy-start.1 = (f32[3,3,512]{2,1,0:T(4,128)S(1)}, f32[3,3,512]{2,1,0:T(4,128)}, u32[]{:S(2)}) copy-start(f32[3,3,512]{2,1,0:T(4,128)} %param.5) | copy-start | bytes 55300
  40.5 5.9 %collective-permute-start = (bf16[4,128,512]{2,1,0:T(8,128)(2,1)S(1)}, bf16[4,128,512]{2,1,0:T(8,128)(2,1)S(1)}, u32[]{:S(2)}, u32[]{:S(2)}) collective-permute-start(bf16[4,128,512]{2,1,0:T(8,128)(2,1)S(1)} %all_gather.3.image_ref), channel_id=1, source_target_pairs={{0,4},{4,0},{1,5},{5,1},{2,6},{6,2},{3,7},{7,3},{8,12},{12,8},{9,1... | collective-permute-start | bytes 1572872 | tf_op jit(solution)/shard_map/ppermute | solution.py:171

commit v5 on v4

--- a/solution.py
+++ b/solution.py
@@ -21,16 +21,6 @@
         scratch_shapes=scratch,
         compiler_params=pltpu.CompilerParams(vmem_limit_bytes=48 * 1024 * 1024),
     )
-
-
-def spread_body(chunk_ref, out_ref, sems):
-    copies = [
-        pltpu.make_async_copy(chunk_ref, out_ref.at[g], sems.at[g]) for g in range(NZ * NY)
-    ]
-    for copy in copies:
-        copy.start()
-    for copy in copies:
-        copy.wait()
 
 
 def convolve(image_ref, wide, rows_ref, z_ref, put):
@@ -158,15 +148,9 @@
 def shards(backbone, conv_weight, smooth_weight):
     image = backbone.reshape(ROWS * COLS, CH)
     chunk = conv_weight.transpose(0, 1, 3, 2).reshape(9, 4, CH)
-    spread = pl.pallas_call(
-        spread_body,
-        out_shape=jax.ShapeDtypeStruct((NZ * NY,) + chunk.shape, BF16),
-        in_specs=[pl.BlockSpec(memory_space=pl.ANY)],
-        out_specs=pl.BlockSpec(memory_space=pl.ANY),
-        scratch_shapes=[pltpu.SemaphoreType.DMA((NZ * NY,))],
-        name="spread",
-    )(chunk)
-    kernels = exchange(spread, ("z", "y"))
+    kernels = exchange(
+        jnp.broadcast_to(chunk[None], (NZ * NY,) + chunk.shape), ("z", "y")
+    )
     own = lax.all_gather(image, "x")
     partner = lax.ppermute(own, "c", [(0, 1), (1, 0)])
     rows = [pltpu.VMEM((4, 512, 128), F32), pltpu.VMEM((5, 18, 48, 128), F32)]

time: 90.6 us -> 73.3 us (0.81)
  Pallas kernels: 22.8 us -> 3.68 us
  local copies, waits for them, and re-layouts: 0.04 us -> 1.78 us
    pallas_call x1 -> x0, Pallas kernels: 19.1 us -> none  [shards(): pl.pallas_call(spread_body, out_shape=jax.ShapeDtypeStruct((NZ * NY,) + c...]
    broadcast_in_dim x0 -> x1, local copies, waits for them, and re-layouts: none -> 1.74 us  [shards(): jnp.broadcast_to(chunk[None], (NZ * NY,) + chunk.shape)]
where the time goes in v5:
time: 73.3 us; the launch traced here: 72.9 us
  blocking collectives  52.8 us (72%)
  starting transfers between devices  14 us (19%)
  Pallas kernels  3.68 us (5%)
  local copies, waits for them, and re-layouts  1.78 us (2%)
    all_to_all x2, blocking collectives, exchange(): return lax.all_to_all(value, axes, 0, 0, tiled=True)  41.2 us
    all_gather x1, blocking collectives, shards(): own = lax.all_gather(image, 'x')  11.6 us
    all_to_all x1, starting transfers between devices, exchange(): return lax.all_to_all(value, axes, 0, 0, tiled=True)  9.68 us
    ppermute x1, starting transfers between devices, shards(): partner = lax.ppermute(own, 'c', [(0, 1), (1, 0)])  4.35 us
    broadcast_in_dim x1, local copies, waits for them, and re-layouts, shards(): jnp.broadcast_to(chunk[None], (NZ * NY,) + chunk.shape)  1.74 us
  transfers between devices with their start and end apart: 2, of which 1 were waited for; matrix products, arithmetic and copies ran while one was open for 0% of the time, Pallas kernels for 1%

profile of v5, /device:TPU:1, one launch (start us, length us, event | category | flops | bytes accessed | tf_op | source)
XLA Modules:
  0.0 72.9 jit_solution(14911904001208422426)
XLA Ops:
  0.0 1.7 %broadcast_in_dim.8 = bf16[16,9,4,512]{3,2,1,0:T(4,128)(2,1)} broadcast(bf16[9,4,512]{2,1,0:T(4,128)(2,1)} %bitcast.16), dimensions={1,2,3} | broadcast | bytes 626688 | tf_op jit(solution)/shard_map/broadcast_in_dim | solution.py:152
  1.7 0.0 copy-start
  1.7 9.7 %all-to-all-start = ((bf16[16,9,4,512]{3,2,1,0:T(4,128)(2,1)}), bf16[16,9,4,512]{3,2,1,0:T(4,128)(2,1)S(1)}, u32[]{:S(2)}, u32[]{:S(2)}) async-start(bf16[16,9,4,512]{3,2,1,0:T(4,128)(2,1)} %broadcast_in_dim.8), calls=%async_computation | async-start | bytes 1179648 | tf_op jit(solution)/shard_map/all_to_all | solution.py:145
  11.4 0.0 copy-done
  11.4 0.0 copy-start.1
  11.5 11.6 %all_gather.3.image_ref = bf16[4,128,512]{2,1,0:T(8,128)(2,1)S(1)} all-gather(bf16[1,128,512]{2,1,0:T(8,128)(2,1)S(1)} %bitcast.15), channel_id=1, replica_groups=mesh['x'=4,'z'=2,'y'=8,'c'=2,'rep'=4] {'x'}, dimensions={0}, use_global_device_ids=true | all-gather | bytes 655360 | tf_op jit(solution)/shard_map/all_gather | solution.py:154
  23.1 4.3 %collective-permute-start = (bf16[4,128,512]{2,1,0:T(8,128)(2,1)S(1)}, bf16[4,128,512]{2,1,0:T(8,128)(2,1)S(1)}, u32[]{:S(2)}, u32[]{:S(2)}) collective-permute-start(bf16[4,128,512]{2,1,0:T(8,128)(2,1)S(1)} %all_gather.3.image_ref), channel_id=1, source_target_pairs={{0,4},{4,0},{1,5},{5,1},{2,6},{6,2},{3,7},{7,3},{8,12},{12,8},{9,1... | collective-permute-start | bytes 1572872 | tf_op jit(solution)/shard_map/ppermute | solution.py:155
  27.5 0.0 copy-done.1
  27.5 0.0 all-to-all-done.weight_ref
  27.5 1.0 %shard_map.37 = (bf16[512,128]{1,0:T(8,128)(2,1)S(1)}, bf16[640,512]{1,0:T(8,128)(2,1)S(1)}) custom-call(bf16[16,9,4,512]{3,2,1,0:T(4,128)(2,1)S(1)} %all-to-all-done.weight_ref, bf16[4,128,512]{2,1,0:T(8,128)(2,1)S(1)} %all_gather.3.image_ref), custom_call_target="tpu_custom_call" | custom-call | tf_op jit(solution)/shard_map/pallas_call | solution.py:158
  28.5 0.5 collective-permute-done.image_ref
  29.0 0.9 %shard_map.38 = bf16[512,128]{1,0:T(8,128)(2,1)S(1)} custom-call(bf16[640,512]{1,0:T(8,128)(2,1)S(1)} %get-tuple-element.9.wide_ref, bf16[4,128,512]{2,1,0:T(8,128)(2,1)S(1)} %collective-permute-done.image_ref, bf16[512,128]{1,0:T(8,128)(2,1)S(1)} %get-tuple-element.10.own_ref), custom_call_target="tpu_custom_call" | custom-call | tf_op jit(solution)/shard_map/pallas_call | solution.py:163
  29.8 24.0 %all_to_all.15 = bf16[128,4,128]{2,1,0:T(4,128)(2,1)S(1)} all-to-all(bf16[128,4,128]{2,1,0:T(4,128)(2,1)S(1)} %bitcast.13), channel_id=1, replica_groups=mesh['x'=4,'z'=2,'y'=8,'c'=2,'rep'=4] {'x','z','y','c'}, dimensions={0} | all-to-all | bytes 262144 | tf_op jit(solution)/shard_map/all_to_all | solution.py:145
  53.9 1.0 %shard_map.39 = bf16[512,128]{1,0:T(8,128)(2,1)S(1)} custom-call(bf16[512,128]{1,0:T(8,128)(2,1)S(1)} %bitcast.11), custom_call_target="tpu_custom_call" | custom-call | tf_op jit(solution)/shard_map/pallas_call | solution.py:167
  54.9 17.1 %all_to_all.16 = bf16[128,4,128]{2,1,0:T(4,128)(2,1)S(1)} all-to-all(bf16[128,4,128]{2,1,0:T(4,128)(2,1)S(1)} %bitcast.12), channel_id=1, replica_groups=mesh['x'=4,'z'=2,'y'=8,'c'=2,'rep'=4] {'x','z','y','c'}, dimensions={0} | all-to-all | bytes 262144 | tf_op jit(solution)/shard_map/all_to_all | solution.py:145
  72.0 0.8 %shard_map.40 = bf16[128,512]{1,0:T(8,128)(2,1)} custom-call(bf16[512,128]{1,0:T(8,128)(2,1)S(1)} %bitcast.10, f32[9,8,128]{2,1,0:T(8,128)S(1)} %bitcast.14), custom_call_target="tpu_custom_call" | custom-call | tf_op jit(solution)/shard_map/pallas_call | solution.py:173
  (2 shorter events, 0.0 us)
Async XLA Ops:
  1.7 9.7 %copy-start = (bf16[1,16,8,512]{3,2,1,0:T(8,128)(2,1)S(1)}, bf16[1,16,8,512]{3,2,1,0:T(8,128)(2,1)}, u32[]{:S(2)}) copy-start(bf16[1,16,8,512]{3,2,1,0:T(8,128)(2,1)} %param.3) | copy-start | bytes 393220
  1.7 25.7 %all-to-all-start = ((bf16[16,9,4,512]{3,2,1,0:T(4,128)(2,1)}), bf16[16,9,4,512]{3,2,1,0:T(4,128)(2,1)S(1)}, u32[]{:S(2)}, u32[]{:S(2)}) async-start(bf16[16,9,4,512]{3,2,1,0:T(4,128)(2,1)} %broadcast_in_dim.8), calls=%async_computation | async-start | bytes 1179648 | tf_op jit(solution)/shard_map/all_to_all | solution.py:145
  11.4 16.0 %copy-start.1 = (f32[3,3,512]{2,1,0:T(4,128)S(1)}, f32[3,3,512]{2,1,0:T(4,128)}, u32[]{:S(2)}) copy-start(f32[3,3,512]{2,1,0:T(4,128)} %param.5) | copy-start | bytes 55300
  23.1 5.9 %collective-permute-start = (bf16[4,128,512]{2,1,0:T(8,128)(2,1)S(1)}, bf16[4,128,512]{2,1,0:T(8,128)(2,1)S(1)}, u32[]{:S(2)}, u32[]{:S(2)}) collective-permute-start(bf16[4,128,512]{2,1,0:T(8,128)(2,1)S(1)} %all_gather.3.image_ref), channel_id=1, source_target_pairs={{0,4},{4,0},{1,5},{5,1},{2,6},{6,2},{3,7},{7,3},{8,12},{12,8},{9,1... | collective-permute-start | bytes 1572872 | tf_op jit(solution)/shard_map/ppermute | solution.py:155

commit v6 on v5

--- a/solution.py
+++ b/solution.py
@@ -119,8 +119,12 @@
     for k in range(NX):
         white = jnp.dot(high, centered[k], preferred_element_type=F32)
         turn_ref[k] = white + jnp.dot(low, centered[k], preferred_element_type=F32)
-        for xs in range(NX):
-            rows_ref[pl.ds(xs * 128 + k, 32, stride=4), :] = turn_ref[k, pl.ds(xs, 32, stride=4), :]
+        for c in range(NC):
+            for r in range(NX):
+                xs = NX - 1 - r if c else r
+                rows_ref[pl.ds(xs * 128 + c * 4 + k, 16, stride=8), :] = turn_ref[
+                    k, pl.ds(c * 4 + r, 16, stride=8), :
+                ]
     out_ref[...] = rows_ref[...].astype(BF16)
 
 
@@ -151,7 +155,8 @@
     kernels = exchange(
         jnp.broadcast_to(chunk[None], (NZ * NY,) + chunk.shape), ("z", "y")
     )
-    own = lax.all_gather(image, "x")
+    ways = [[2 * i for i in range(NX)], [2 * i + 1 for i in reversed(range(NX))]]
+    own = lax.all_gather(image, ("x", "c"), axis_index_groups=ways)
     partner = lax.ppermute(own, "c", [(0, 1), (1, 0)])
     rows = [pltpu.VMEM((4, 512, 128), F32), pltpu.VMEM((5, 18, 48, 128), F32)]
     half = jax.ShapeDtypeStruct((512, 128), BF16)

time: 73.3 us -> 73.3 us (level)
  no operation moved by 1% of the time
where the time goes in v6:
time: 73.3 us; the launch traced here: 72.9 us
  blocking collectives  52.8 us (72%)
  starting transfers between devices  14 us (19%)
  Pallas kernels  3.71 us (5%)
  local copies, waits for them, and re-layouts  1.78 us (2%)
    all_to_all x2, blocking collectives, exchange(): return lax.all_to_all(value, axes, 0, 0, tiled=True)  41.2 us
    all_gather x1, blocking collectives, shards(): own = lax.all_gather(image, ('x', 'c'), axis_index_groups=ways)  11.7 us
    all_to_all x1, starting transfers between devices, exchange(): return lax.all_to_all(value, axes, 0, 0, tiled=True)  9.68 us
    ppermute x1, starting transfers between devices, shards(): partner = lax.ppermute(own, 'c', [(0, 1), (1, 0)])  4.33 us
    broadcast_in_dim x1, local copies, waits for them, and re-layouts, shards(): jnp.broadcast_to(chunk[None], (NZ * NY,) + chunk.shape)  1.74 us
  transfers between devices with their start and end apart: 2, of which 1 were waited for; matrix products, arithmetic and copies ran while one was open for 0% of the time, Pallas kernels for 1%

profile of v6, /device:TPU:1, one launch (start us, length us, event | category | flops | bytes accessed | tf_op | source)
XLA Modules:
  0.0 72.9 jit_solution(7032462680666891452)
XLA Ops:
  0.0 1.7 %broadcast_in_dim.8 = bf16[16,9,4,512]{3,2,1,0:T(4,128)(2,1)} broadcast(bf16[9,4,512]{2,1,0:T(4,128)(2,1)} %bitcast.16), dimensions={1,2,3} | broadcast | bytes 626688 | tf_op jit(solution)/shard_map/broadcast_in_dim | solution.py:156
  1.7 0.0 copy-start
  1.7 9.7 %all-to-all-start = ((bf16[16,9,4,512]{3,2,1,0:T(4,128)(2,1)}), bf16[16,9,4,512]{3,2,1,0:T(4,128)(2,1)S(1)}, u32[]{:S(2)}, u32[]{:S(2)}) async-start(bf16[16,9,4,512]{3,2,1,0:T(4,128)(2,1)} %broadcast_in_dim.8), calls=%async_computation | async-start | bytes 1179648 | tf_op jit(solution)/shard_map/all_to_all | solution.py:149
  11.4 0.0 copy-done
  11.4 0.0 copy-start.1
  11.5 11.7 %all_gather.3.image_ref = bf16[4,128,512]{2,1,0:T(8,128)(2,1)S(1)} all-gather(bf16[1,128,512]{2,1,0:T(8,128)(2,1)S(1)} %bitcast.15), channel_id=1, replica_groups={{0,128,256,384},{388,260,132,4},{1,129,257,385},{389,261,133,5},{2,130,..., dimensions={0}, use_global_device_ids=true | all-gather | bytes 655360 | tf_op jit(solution)/shard_map/all_gather | solution.py:159
  23.1 4.3 %collective-permute-start = (bf16[4,128,512]{2,1,0:T(8,128)(2,1)S(1)}, bf16[4,128,512]{2,1,0:T(8,128)(2,1)S(1)}, u32[]{:S(2)}, u32[]{:S(2)}) collective-permute-start(bf16[4,128,512]{2,1,0:T(8,128)(2,1)S(1)} %all_gather.3.image_ref), channel_id=1, source_target_pairs={{0,4},{4,0},{1,5},{5,1},{2,6},{6,2},{3,7},{7,3},{8,12},{12,8},{9,1... | collective-permute-start | bytes 1572872 | tf_op jit(solution)/shard_map/ppermute | solution.py:160
  27.5 0.0 copy-done.1
  27.5 0.0 all-to-all-done.weight_ref
  27.5 1.0 %shard_map.37 = (bf16[512,128]{1,0:T(8,128)(2,1)S(1)}, bf16[640,512]{1,0:T(8,128)(2,1)S(1)}) custom-call(bf16[16,9,4,512]{3,2,1,0:T(4,128)(2,1)S(1)} %all-to-all-done.weight_ref, bf16[4,128,512]{2,1,0:T(8,128)(2,1)S(1)} %all_gather.3.image_ref), custom_call_target="tpu_custom_call" | custom-call | tf_op jit(solution)/shard_map/pallas_call | solution.py:163
  28.5 0.5 collective-permute-done.image_ref
  29.0 0.9 %shard_map.38 = bf16[512,128]{1,0:T(8,128)(2,1)S(1)} custom-call(bf16[640,512]{1,0:T(8,128)(2,1)S(1)} %get-tuple-element.9.wide_ref, bf16[4,128,512]{2,1,0:T(8,128)(2,1)S(1)} %collective-permute-done.image_ref, bf16[512,128]{1,0:T(8,128)(2,1)S(1)} %get-tuple-element.10.own_ref), custom_call_target="tpu_custom_call" | custom-call | tf_op jit(solution)/shard_map/pallas_call | solution.py:168
  29.8 24.0 %all_to_all.15 = bf16[128,4,128]{2,1,0:T(4,128)(2,1)S(1)} all-to-all(bf16[128,4,128]{2,1,0:T(4,128)(2,1)S(1)} %bitcast.13), channel_id=1, replica_groups=mesh['x'=4,'z'=2,'y'=8,'c'=2,'rep'=4] {'x','z','y','c'}, dimensions={0} | all-to-all | bytes 262144 | tf_op jit(solution)/shard_map/all_to_all | solution.py:149
  53.9 1.0 %shard_map.39 = bf16[512,128]{1,0:T(8,128)(2,1)S(1)} custom-call(bf16[512,128]{1,0:T(8,128)(2,1)S(1)} %bitcast.11), custom_call_target="tpu_custom_call" | custom-call | tf_op jit(solution)/shard_map/pallas_call | solution.py:172
  54.9 17.1 %all_to_all.16 = bf16[128,4,128]{2,1,0:T(4,128)(2,1)S(1)} all-to-all(bf16[128,4,128]{2,1,0:T(4,128)(2,1)S(1)} %bitcast.12), channel_id=1, replica_groups=mesh['x'=4,'z'=2,'y'=8,'c'=2,'rep'=4] {'x','z','y','c'}, dimensions={0} | all-to-all | bytes 262144 | tf_op jit(solution)/shard_map/all_to_all | solution.py:149
  72.1 0.8 %shard_map.40 = bf16[128,512]{1,0:T(8,128)(2,1)} custom-call(bf16[512,128]{1,0:T(8,128)(2,1)S(1)} %bitcast.10, f32[9,8,128]{2,1,0:T(8,128)S(1)} %bitcast.14), custom_call_target="tpu_custom_call" | custom-call | tf_op jit(solution)/shard_map/pallas_call | solution.py:178
  (2 shorter events, 0.0 us)
Async XLA Ops:
  1.7 9.7 %copy-start = (bf16[1,16,8,512]{3,2,1,0:T(8,128)(2,1)S(1)}, bf16[1,16,8,512]{3,2,1,0:T(8,128)(2,1)}, u32[]{:S(2)}) copy-start(bf16[1,16,8,512]{3,2,1,0:T(8,128)(2,1)} %param.3) | copy-start | bytes 393220
  1.7 25.7 %all-to-all-start = ((bf16[16,9,4,512]{3,2,1,0:T(4,128)(2,1)}), bf16[16,9,4,512]{3,2,1,0:T(4,128)(2,1)S(1)}, u32[]{:S(2)}, u32[]{:S(2)}) async-start(bf16[16,9,4,512]{3,2,1,0:T(4,128)(2,1)} %broadcast_in_dim.8), calls=%async_computation | async-start | bytes 1179648 | tf_op jit(solution)/shard_map/all_to_all | solution.py:149
  11.4 16.0 %copy-start.1 = (f32[3,3,512]{2,1,0:T(4,128)S(1)}, f32[3,3,512]{2,1,0:T(4,128)}, u32[]{:S(2)}) copy-start(f32[3,3,512]{2,1,0:T(4,128)} %param.5) | copy-start | bytes 55300
  23.1 5.9 %collective-permute-start = (bf16[4,128,512]{2,1,0:T(8,128)(2,1)S(1)}, bf16[4,128,512]{2,1,0:T(8,128)(2,1)S(1)}, u32[]{:S(2)}, u32[]{:S(2)}) collective-permute-start(bf16[4,128,512]{2,1,0:T(8,128)(2,1)S(1)} %all_gather.3.image_ref), channel_id=1, source_target_pairs={{0,4},{4,0},{1,5},{5,1},{2,6},{6,2},{3,7},{7,3},{8,12},{12,8},{9,1... | collective-permute-start | bytes 1572872 | tf_op jit(solution)/shard_map/ppermute | solution.py:160

commit v7 on v5

--- a/solution.py
+++ b/solution.py
@@ -23,11 +23,11 @@
     )
 
 
-def convolve(image_ref, wide, rows_ref, z_ref, put):
+def convolve(image_ref, half, wide, rows_ref, z_ref, put):
     for t in range(4):
         for j in range(NX):
             rows_ref[t, pl.ds(j, IMAGES, stride=4), :] = image_ref[
-                j, :, t * 128 : (t + 1) * 128
+                NZ * j + half, :, t * 128 : (t + 1) * 128
             ].astype(F32)
     x = jnp.concatenate([rows_ref[t].astype(BF16) for t in range(4)], axis=1)
     z_ref[:, 0] = jnp.zeros((5, 48, 128), F32)
@@ -44,32 +44,32 @@
             a, b = t // 3, t % 3
             piece = z_ref[t // 2, h + a, 4 + 4 * b : 36 + 4 * b, :]
             sums[t % 2] = piece if sums[t % 2] is None else sums[t % 2] + piece
-        put(h, sums[0] + pltpu.roll(sums[1], 124, 1))
+        put(h, sums[0] + pltpu.roll(sums[1], 64, 1))
 
 
-def conv_own_body(weight_ref, image_ref, out_ref, wide_ref, tall_ref, rows_ref, z_ref):
-    tall_ref[512:640, :] = jnp.zeros((128, CH), F32)
+def conv_first_body(weight_ref, image_ref, out_ref, wide_ref, tall_ref, rows_ref, z_ref):
+    tall_ref[576:640, :] = jnp.zeros((64, CH), F32)
     for t in range(9):
-        for g in range(NZ * NY):
-            at = (t // 2) * 128 + g * 8 + (t % 2) * 4
+        for g in range(NY * NC):
+            at = t * 64 + g * 4
             tall_ref[at : at + 4, :] = weight_ref[g, t].astype(F32)
     wide_ref[...] = tall_ref[...].astype(BF16)
 
     def put(h, total):
         out_ref[h * 32 : (h + 1) * 32, :] = total.astype(BF16)
 
-    convolve(image_ref, lambda lo, hi: wide_ref[lo:hi, :], rows_ref, z_ref, put)
+    convolve(image_ref, 0, lambda lo, hi: wide_ref[lo:hi, :], rows_ref, z_ref, put)
 
 
-def conv_partner_body(wide_ref, image_ref, own_ref, out_ref, rows_ref, z_ref):
-    slot0 = lax.broadcasted_iota(jnp.int32, (32, 128), 1) % 8 < 4
+def conv_second_body(wide_ref, image_ref, own_ref, out_ref, rows_ref, z_ref):
+    lane_lo = lax.broadcasted_iota(jnp.int32, (32, 128), 1) < 64
 
     def put(h, total):
         own = own_ref[h * 32 : (h + 1) * 32, :].astype(F32)
-        merged = jnp.where(slot0, own, pltpu.roll(total, 4, 1))
+        merged = jnp.where(lane_lo, own, pltpu.roll(total, 64, 1))
         out_ref[h * 32 : (h + 1) * 32, :] = merged.astype(BF16)
 
-    convolve(image_ref, lambda lo, hi: wide_ref[lo:hi, :], rows_ref, z_ref, put)
+    convolve(image_ref, 1, lambda lo, hi: wide_ref[lo:hi, :], rows_ref, z_ref, put)
 
 
 def split(a):
@@ -85,9 +85,7 @@
 
 
 def stats_body(got_ref, out_ref, turn_ref, rows_ref):
-    tiles = (16, 8, 128)
-    slot0 = lax.broadcasted_iota(jnp.int32, tiles, 2) % 8 < 4
-    row_lo = lax.broadcasted_iota(jnp.int32, tiles, 1) < 4
+    lane_lo = lax.broadcasted_iota(jnp.int32, (64, 128), 1) < 64
     eye = (
         lax.broadcasted_iota(jnp.int32, (IMAGES, IMAGES), 0)
         == lax.broadcasted_iota(jnp.int32, (IMAGES, IMAGES), 1)
@@ -95,10 +93,11 @@
     centered = []
     gram = None
     for k in range(NX):
-        v = got_ref[k * 128 : (k + 1) * 128, :].astype(F32).reshape(tiles)
-        mixed = jnp.where(slot0, v, pltpu.roll(v, 4, 1))
-        turned = jnp.where(slot0, pltpu.roll(mixed, 124, 2), pltpu.roll(mixed, 4, 2))
-        x = jnp.where(row_lo, mixed, turned).reshape(IMAGES, 128)
+        z0 = got_ref[k * 128 : k * 128 + 64, :].astype(F32)
+        z1 = got_ref[k * 128 + 64 : (k + 1) * 128, :].astype(F32)
+        even = jnp.where(lane_lo, z0, pltpu.roll(z1, 64, 1))
+        odd = jnp.where(lane_lo, pltpu.roll(z0, 64, 1), z1)
+        x = jnp.concatenate([even, odd], axis=0)
         center = jnp.sum(x, axis=0, keepdims=True) / IMAGES
         x = (x - center).astype(BF16)
         centered.append(x)
@@ -148,19 +147,16 @@
 def shards(backbone, conv_weight, smooth_weight):
     image = backbone.reshape(ROWS * COLS, CH)
     chunk = conv_weight.transpose(0, 1, 3, 2).reshape(9, 4, CH)
-    kernels = exchange(
-        jnp.broadcast_to(chunk[None], (NZ * NY,) + chunk.shape), ("z", "y")
-    )
-    own = lax.all_gather(image, "x")
-    partner = lax.ppermute(own, "c", [(0, 1), (1, 0)])
+    images = exchange(jnp.broadcast_to(image[None], (NX * NZ,) + image.shape), ("x", "z"))
+    kernels = lax.all_gather(chunk, ("y", "c"))
     rows = [pltpu.VMEM((4, 512, 128), F32), pltpu.VMEM((5, 18, 48, 128), F32)]
     half = jax.ShapeDtypeStruct((512, 128), BF16)
     first, wide = vmem_call(
-        conv_own_body,
+        conv_first_body,
         (half, jax.ShapeDtypeStruct((640, CH), BF16)),
         [pltpu.VMEM((640, CH), F32)] + rows,
-    )(kernels, own)
-    features = vmem_call(conv_partner_body, half, rows)(wide, partner, first)
+    )(kernels, images)
+    features = vmem_call(conv_second_body, half, rows)(wide, images, first)
     taps = jnp.tile(smooth_weight.reshape(9, 4, 128), (1, 2, 1))
     features, taps = lax.optimization_barrier((features, taps))
     got = exchange(features.reshape(128, 4, 128), AXES)

time: 73.3 us -> 72.3 us (0.986)
  starting transfers between devices: 14 us -> 6.78 us
  blocking collectives: 52.8 us -> 58.7 us
  local copies, waits for them, and re-layouts: 1.78 us -> 2.73 us
    all_gather x1, blocking collectives: 11.6 us -> 20 us  [shards(): kernels = lax.all_gather(chunk, ('y', 'c'))]
    ppermute x1 -> x0, starting transfers between devices: 4.35 us -> none  [shards(): partner = lax.ppermute(own, 'c', [(0, 1), (1, 0)])]
    all_to_all x1, starting transfers between devices: 9.68 us -> 6.78 us  [exchange(): return lax.all_to_all(value, axes, 0, 0, tiled=True)]
    all_to_all x2, blocking collectives: 41.2 us -> 38.7 us  [exchange(): return lax.all_to_all(value, axes, 0, 0, tiled=True)]
  transfers between devices with their start and end apart: 2 -> 1, of which waited for: 1 -> 0; matrix products, arithmetic and copies ran while one was open for 0% -> 0% of each run, Pallas kernels for 1% -> 0%
where the time goes in v7:
time: 72.3 us; the launch traced here: 71.9 us
  blocking collectives  58.7 us (81%)
  starting transfers between devices  6.78 us (9%)
  Pallas kernels  3.67 us (5%)
  local copies, waits for them, and re-layouts  2.73 us (4%)
    all_to_all x2, blocking collectives, exchange(): return lax.all_to_all(value, axes, 0, 0, tiled=True)  38.7 us
    all_gather x1, blocking collectives, shards(): kernels = lax.all_gather(chunk, ('y', 'c'))  20 us
    all_to_all x1, starting transfers between devices, exchange(): return lax.all_to_all(value, axes, 0, 0, tiled=True)  6.78 us
    broadcast_in_dim x1, local copies, waits for them, and re-layouts, shards(): jnp.broadcast_to(image[None], (NX * NZ,) + image.shape)  1.96 us
  transfers between devices with their start and end apart: 1, of which 0 were waited for; matrix products, arithmetic and copies ran while one was open for 0% of the time, Pallas kernels for 0%

profile of v7, /device:TPU:1, one launch (start us, length us, event | category | flops | bytes accessed | tf_op | source)
XLA Modules:
  0.0 71.9 jit_solution(15401677030956761672)
XLA Ops:
  0.0 2.0 %broadcast_in_dim.8 = bf16[8,128,512]{2,1,0:T(8,128)(2,1)} broadcast(bf16[128,512]{1,0:T(8,128)(2,1)} %bitcast.15), dimensions={1,2} | broadcast | bytes 1179648 | tf_op jit(solution)/shard_map/broadcast_in_dim | solution.py:150
  2.0 0.0 copy-start.1
  2.0 6.8 %all-to-all-start = ((bf16[8,128,512]{2,1,0:T(8,128)(2,1)}), bf16[8,128,512]{2,1,0:T(8,128)(2,1)S(1)}, u32[]{:S(2)}, u32[]{:S(2)}) async-start(bf16[8,128,512]{2,1,0:T(8,128)(2,1)} %broadcast_in_dim.8), calls=%async_computation | async-start | bytes 2097152 | tf_op jit(solution)/shard_map/all_to_all | solution.py:144
  8.7 0.0 copy-done.1
  8.7 0.0 copy-start
  8.8 0.7 %copy-done = bf16[3,3,512,4]{2,3,1,0:T(4,128)(2,1)S(1)} copy-done((bf16[3,3,512,4]{2,3,1,0:T(4,128)(2,1)S(1)}, bf16[3,3,512,4]{2,3,1,0:T(4,128)(2,1)}, u32[]{:S(2)}) %copy-start) | copy-done | bytes 36888
  9.5 20.0 %all_gather.3.weight_ref = bf16[16,9,4,512]{3,2,1,0:T(4,128)(2,1)S(1)} all-gather(bf16[1,9,4,512]{3,2,1,0:T(4,128)(2,1)S(1)} %bitcast.16), channel_id=1, replica_groups=mesh['x'=4,'z'=2,'y'=8,'c'=2,'rep'=4] {'y','c'}, dimensions={0}, use_global_device_ids=true | all-gather | bytes 626688 | tf_op jit(solution)/shard_map/all_gather | solution.py:151
  29.5 0.0 all-to-all-done.image_ref
  29.5 1.0 %shard_map.37 = (bf16[512,128]{1,0:T(8,128)(2,1)S(1)}, bf16[640,512]{1,0:T(8,128)(2,1)S(1)}) custom-call(bf16[16,9,4,512]{3,2,1,0:T(4,128)(2,1)S(1)} %all_gather.3.weight_ref, bf16[8,128,512]{2,1,0:T(8,128)(2,1)S(1)} %all-to-all-done.image_ref), custom_call_target="tpu_custom_call" | custom-call | tf_op jit(solution)/shard_map/pallas_call | solution.py:154
  30.5 0.9 %shard_map.38 = bf16[512,128]{1,0:T(8,128)(2,1)S(1)} custom-call(bf16[640,512]{1,0:T(8,128)(2,1)S(1)} %get-tuple-element.9.wide_ref, bf16[8,128,512]{2,1,0:T(8,128)(2,1)S(1)} %all-to-all-done.image_ref, bf16[512,128]{1,0:T(8,128)(2,1)S(1)} %get-tuple-element.10.own_ref), custom_call_target="tpu_custom_call" | custom-call | tf_op jit(solution)/shard_map/pallas_call | solution.py:159
  31.3 21.6 %all_to_all.15 = bf16[128,4,128]{2,1,0:T(4,128)(2,1)S(1)} all-to-all(bf16[128,4,128]{2,1,0:T(4,128)(2,1)S(1)} %bitcast.13), channel_id=1, replica_groups=mesh['x'=4,'z'=2,'y'=8,'c'=2,'rep'=4] {'x','z','y','c'}, dimensions={0} | all-to-all | bytes 262144 | tf_op jit(solution)/shard_map/all_to_all | solution.py:144
  52.9 1.0 %shard_map.39 = bf16[512,128]{1,0:T(8,128)(2,1)S(1)} custom-call(bf16[512,128]{1,0:T(8,128)(2,1)S(1)} %bitcast.11), custom_call_target="tpu_custom_call" | custom-call | tf_op jit(solution)/shard_map/pallas_call | solution.py:163
  53.9 17.1 %all_to_all.16 = bf16[128,4,128]{2,1,0:T(4,128)(2,1)S(1)} all-to-all(bf16[128,4,128]{2,1,0:T(4,128)(2,1)S(1)} %bitcast.12), channel_id=1, replica_groups=mesh['x'=4,'z'=2,'y'=8,'c'=2,'rep'=4] {'x','z','y','c'}, dimensions={0} | all-to-all | bytes 262144 | tf_op jit(solution)/shard_map/all_to_all | solution.py:144
  71.1 0.8 %shard_map.40 = bf16[128,512]{1,0:T(8,128)(2,1)} custom-call(bf16[512,128]{1,0:T(8,128)(2,1)S(1)} %bitcast.10, f32[9,8,128]{2,1,0:T(8,128)S(1)} %bitcast.14), custom_call_target="tpu_custom_call" | custom-call | tf_op jit(solution)/shard_map/pallas_call | solution.py:169
  (2 shorter events, 0.0 us)
Async XLA Ops:
  2.0 6.8 %copy-start.1 = (f32[3,3,512]{2,1,0:T(4,128)S(1)}, f32[3,3,512]{2,1,0:T(4,128)}, u32[]{:S(2)}) copy-start(f32[3,3,512]{2,1,0:T(4,128)} %param.5) | copy-start | bytes 55300
  2.0 27.5 %all-to-all-start = ((bf16[8,128,512]{2,1,0:T(8,128)(2,1)}), bf16[8,128,512]{2,1,0:T(8,128)(2,1)S(1)}, u32[]{:S(2)}, u32[]{:S(2)}) async-start(bf16[8,128,512]{2,1,0:T(8,128)(2,1)} %broadcast_in_dim.8), calls=%async_computation | async-start | bytes 2097152 | tf_op jit(solution)/shard_map/all_to_all | solution.py:144
  8.7 0.8 %copy-start = (bf16[3,3,512,4]{2,3,1,0:T(4,128)(2,1)S(1)}, bf16[3,3,512,4]{2,3,1,0:T(4,128)(2,1)}, u32[]{:S(2)}) copy-start(bf16[3,3,512,4]{2,3,1,0:T(4,128)(2,1)} %param.4) | copy-start | bytes 110596

commit v8 on v7

--- a/solution.py
+++ b/solution.py
@@ -23,53 +23,44 @@
     )
 
 
-def convolve(image_ref, half, wide, rows_ref, z_ref, put):
-    for t in range(4):
-        for j in range(NX):
-            rows_ref[t, pl.ds(j, IMAGES, stride=4), :] = image_ref[
-                NZ * j + half, :, t * 128 : (t + 1) * 128
-            ].astype(F32)
-    x = jnp.concatenate([rows_ref[t].astype(BF16) for t in range(4)], axis=1)
-    z_ref[:, 0] = jnp.zeros((5, 48, 128), F32)
-    z_ref[:, 17] = jnp.zeros((5, 48, 128), F32)
-    z_ref[:, :, 0:8] = jnp.zeros((5, 18, 8, 128), F32)
-    z_ref[:, :, 40:48] = jnp.zeros((5, 18, 8, 128), F32)
-    for lo, hi in ((0, 256), (256, 512), (512, 640)):
-        part = lax.dot_general(x, wide(lo, hi), NT, preferred_element_type=F32)
-        for at in range(lo, hi, 128):
-            z_ref[at // 128, 1:17, 8:40] = part[:, at - lo : at - lo + 128].reshape(ROWS, 32, 128)
-    for h in range(ROWS):
-        sums = [None, None]
-        for t in range(9):
-            a, b = t // 3, t % 3
-            piece = z_ref[t // 2, h + a, 4 + 4 * b : 36 + 4 * b, :]
-            sums[t % 2] = piece if sums[t % 2] is None else sums[t % 2] + piece
-        put(h, sums[0] + pltpu.roll(sums[1], 64, 1))
-
-
-def conv_first_body(weight_ref, image_ref, out_ref, wide_ref, tall_ref, rows_ref, z_ref):
+def conv_body(weight_ref, image_ref, out_ref, tall_ref, z_ref, rows_ref):
     tall_ref[576:640, :] = jnp.zeros((64, CH), F32)
     for t in range(9):
         for g in range(NY * NC):
             at = t * 64 + g * 4
             tall_ref[at : at + 4, :] = weight_ref[g, t].astype(F32)
-    wide_ref[...] = tall_ref[...].astype(BF16)
-
-    def put(h, total):
-        out_ref[h * 32 : (h + 1) * 32, :] = total.astype(BF16)
-
-    convolve(image_ref, 0, lambda lo, hi: wide_ref[lo:hi, :], rows_ref, z_ref, put)
-
-
-def conv_second_body(wide_ref, image_ref, own_ref, out_ref, rows_ref, z_ref):
+    group = NX * NZ
+    z_ref[:, :, 0:16] = jnp.zeros((5, group, 16, 128), F32)
+    z_ref[:, :, 144:160] = jnp.zeros((5, group, 16, 128), F32)
+    x = image_ref[...].reshape(group * ROWS * COLS, CH)
+    for lo, hi in ((0, 256), (256, 512), (512, 640)):
+        wide = tall_ref[lo:hi, :].astype(BF16)
+        part = lax.dot_general(x, wide, NT, preferred_element_type=F32)
+        for at in range(lo, hi, 128):
+            z_ref[at // 128, :, 16:144] = part[:, at - lo : at - lo + 128].reshape(group, 128, 128)
     lane_lo = lax.broadcasted_iota(jnp.int32, (32, 128), 1) < 64
-
-    def put(h, total):
-        own = own_ref[h * 32 : (h + 1) * 32, :].astype(F32)
-        merged = jnp.where(lane_lo, own, pltpu.roll(total, 64, 1))
-        out_ref[h * 32 : (h + 1) * 32, :] = merged.astype(BF16)
-
-    convolve(image_ref, 1, lambda lo, hi: wide_ref[lo:hi, :], rows_ref, z_ref, put)
+    column = lax.broadcasted_iota(jnp.int32, (32, 128), 0) % COLS
+    inside = (column > 0, None, column < COLS - 1)
+    for j in range(NX):
+        for start in range(0, 128, 32):
+            halves = []
+            for half in range(NZ):
+                sums = [0.0, 0.0]
+                for b in range(3):
+                    parts = [None, None]
+                    for a in range(3):
+                        t = 3 * a + b
+                        at = 16 + start + 8 * (a - 1) + b - 1
+                        piece = z_ref[t // 2, NZ * j + half, at : at + 32, :]
+                        parts[t % 2] = piece if parts[t % 2] is None else parts[t % 2] + piece
+                    for parity in range(2):
+                        part = parts[parity]
+                        if inside[b] is not None:
+                            part = jnp.where(inside[b], part, 0.0)
+                        sums[parity] = sums[parity] + part
+                halves.append(sums[half] + pltpu.roll(sums[1 - half], 64, 1))
+            rows_ref[pl.ds(4 * start + j, 32, stride=4), :] = jnp.where(lane_lo, *halves)
+    out_ref[...] = rows_ref[...].astype(BF16)
 
 
 def split(a):
@@ -147,17 +138,21 @@
 def shards(backbone, conv_weight, smooth_weight):
     image = backbone.reshape(ROWS * COLS, CH)
     chunk = conv_weight.transpose(0, 1, 3, 2).reshape(9, 4, CH)
-    images = exchange(jnp.broadcast_to(image[None], (NX * NZ,) + image.shape), ("x", "z"))
+    group = NX * NZ
+    spread = jnp.broadcast_to(image[None], (group,) + image.shape)
+    images = exchange(spread, ("x", "z"))
     kernels = lax.all_gather(chunk, ("y", "c"))
-    rows = [pltpu.VMEM((4, 512, 128), F32), pltpu.VMEM((5, 18, 48, 128), F32)]
-    half = jax.ShapeDtypeStruct((512, 128), BF16)
-    first, wide = vmem_call(
-        conv_first_body,
-        (half, jax.ShapeDtypeStruct((640, CH), BF16)),
-        [pltpu.VMEM((640, CH), F32)] + rows,
+    kernels, smooth_weight = lax.optimization_barrier((kernels, smooth_weight))
+    taps = jnp.tile(smooth_weight.reshape(9, 4, 128), (1, 2, 1))
+    features = vmem_call(
+        conv_body,
+        jax.ShapeDtypeStruct((512, 128), BF16),
+        [
+            pltpu.VMEM((640, CH), F32),
+            pltpu.VMEM((5, group, 160, 128), F32),
+            pltpu.VMEM((512, 128), F32),
+        ],
     )(kernels, images)
-    features = vmem_call(conv_second_body, half, rows)(wide, images, first)
-    taps = jnp.tile(smooth_weight.reshape(9, 4, 128), (1, 2, 1))
     features, taps = lax.optimization_barrier((features, taps))
     got = exchange(features.reshape(128, 4, 128), AXES)
     white = vmem_call(

time: 72.3 us -> 71 us (0.982)
  local copies, waits for them, and re-layouts: 2.73 us -> 2 us
    unnamed x4, local copies, waits for them, and re-layouts: 0.74 us -> 0.01 us
    pallas_call x2 -> x1, Pallas kernels: 1.83 us -> 1.3 us  [shards(): vmem_call(conv_body, jax.ShapeDtypeStruct((512, 128), BF16), [pltpu.VMEM(...]
where the time goes in v8:
time: 71 us; the launch traced here: 70.7 us
  blocking collectives  58.7 us (83%)
  starting transfers between devices  6.78 us (10%)
  Pallas kernels  3.15 us (4%)
  local copies, waits for them, and re-layouts  2 us (3%)
    all_to_all x2, blocking collectives, exchange(): return lax.all_to_all(value, axes, 0, 0, tiled=True)  38.7 us
    all_gather x1, blocking collectives, shards(): kernels = lax.all_gather(chunk, ('y', 'c'))  20 us
    all_to_all x1, starting transfers between devices, exchange(): return lax.all_to_all(value, axes, 0, 0, tiled=True)  6.78 us
    broadcast_in_dim x1, local copies, waits for them, and re-layouts, shards(): spread = jnp.broadcast_to(image[None], (group,) + image.shape)  1.96 us
  transfers between devices with their start and end apart: 1, of which 0 were waited for; matrix products, arithmetic and copies ran while one was open for 0% of the time, Pallas kernels for 0%

profile of v8, /device:TPU:1, one launch (start us, length us, event | category | flops | bytes accessed | tf_op | source)
XLA Modules:
  0.0 70.7 jit_solution(1247324687318428343)
XLA Ops:
  0.0 2.0 %broadcast_in_dim.8 = bf16[8,128,512]{2,1,0:T(8,128)(2,1)} broadcast(bf16[128,512]{1,0:T(8,128)(2,1)} %bitcast.15), dimensions={1,2} | broadcast | bytes 1179648 | tf_op jit(solution)/shard_map/broadcast_in_dim | solution.py:142
  2.0 0.0 copy-start
  2.0 6.8 %all-to-all-start = ((bf16[8,128,512]{2,1,0:T(8,128)(2,1)}), bf16[8,128,512]{2,1,0:T(8,128)(2,1)S(1)}, u32[]{:S(2)}, u32[]{:S(2)}) async-start(bf16[8,128,512]{2,1,0:T(8,128)(2,1)} %broadcast_in_dim.8), calls=%async_computation | async-start | bytes 2097152 | tf_op jit(solution)/shard_map/all_to_all | solution.py:135
  8.7 0.0 copy-done
  8.7 0.0 copy-start.1
  8.8 20.0 %all_gather.3.weight_ref = bf16[16,9,4,512]{3,2,1,0:T(4,128)(2,1)S(1)} all-gather(bf16[1,9,4,512]{3,2,1,0:T(4,128)(2,1)S(1)} %bitcast.16), channel_id=1, replica_groups=mesh['x'=4,'z'=2,'y'=8,'c'=2,'rep'=4] {'y','c'}, dimensions={0}, use_global_device_ids=true | all-gather | bytes 626688 | tf_op jit(solution)/shard_map/all_gather | solution.py:144
  28.8 0.0 copy-done.1
  28.8 0.0 all-to-all-done.image_ref
  28.8 1.3 %shard_map.37 = bf16[512,128]{1,0:T(8,128)(2,1)S(1)} custom-call(bf16[16,9,4,512]{3,2,1,0:T(4,128)(2,1)S(1)} %all_gather.3.weight_ref, bf16[8,128,512]{2,1,0:T(8,128)(2,1)S(1)} %all-to-all-done.image_ref), custom_call_target="tpu_custom_call" | custom-call | tf_op jit(solution)/shard_map/pallas_call | solution.py:147
  30.1 21.6 %all_to_all.15 = bf16[128,4,128]{2,1,0:T(4,128)(2,1)S(1)} all-to-all(bf16[128,4,128]{2,1,0:T(4,128)(2,1)S(1)} %bitcast.10), channel_id=1, replica_groups=mesh['x'=4,'z'=2,'y'=8,'c'=2,'rep'=4] {'x','z','y','c'}, dimensions={0} | all-to-all | bytes 262144 | tf_op jit(solution)/shard_map/all_to_all | solution.py:135
  51.7 1.0 %shard_map.38 = bf16[512,128]{1,0:T(8,128)(2,1)S(1)} custom-call(bf16[512,128]{1,0:T(8,128)(2,1)S(1)} %bitcast.12), custom_call_target="tpu_custom_call" | custom-call | tf_op jit(solution)/shard_map/pallas_call | solution.py:158
  52.7 17.1 %all_to_all.16 = bf16[128,4,128]{2,1,0:T(4,128)(2,1)S(1)} all-to-all(bf16[128,4,128]{2,1,0:T(4,128)(2,1)S(1)} %bitcast.13), channel_id=1, replica_groups=mesh['x'=4,'z'=2,'y'=8,'c'=2,'rep'=4] {'x','z','y','c'}, dimensions={0} | all-to-all | bytes 262144 | tf_op jit(solution)/shard_map/all_to_all | solution.py:135
  69.8 0.8 %shard_map.39 = bf16[128,512]{1,0:T(8,128)(2,1)} custom-call(bf16[512,128]{1,0:T(8,128)(2,1)S(1)} %bitcast.11, f32[9,8,128]{2,1,0:T(8,128)S(1)} %bitcast.14), custom_call_target="tpu_custom_call" | custom-call | tf_op jit(solution)/shard_map/pallas_call | solution.py:164
  (2 shorter events, 0.0 us)
Async XLA Ops:
  2.0 6.8 %copy-start = (bf16[3,3,512,4]{2,3,1,0:T(4,128)(2,1)S(1)}, bf16[3,3,512,4]{2,3,1,0:T(4,128)(2,1)}, u32[]{:S(2)}) copy-start(bf16[3,3,512,4]{2,3,1,0:T(4,128)(2,1)} %param.4) | copy-start | bytes 110596
  2.0 26.8 %all-to-all-start = ((bf16[8,128,512]{2,1,0:T(8,128)(2,1)}), bf16[8,128,512]{2,1,0:T(8,128)(2,1)S(1)}, u32[]{:S(2)}, u32[]{:S(2)}) async-start(bf16[8,128,512]{2,1,0:T(8,128)(2,1)} %broadcast_in_dim.8), calls=%async_computation | async-start | bytes 2097152 | tf_op jit(solution)/shard_map/all_to_all | solution.py:135
  8.7 20.0 %copy-start.1 = (f32[3,3,512]{2,1,0:T(4,128)S(1)}, f32[3,3,512]{2,1,0:T(4,128)}, u32[]{:S(2)}) copy-start(f32[3,3,512]{2,1,0:T(4,128)} %param.5) | copy-start | bytes 55300

commit v9 on v8

--- a/solution.py
+++ b/solution.py
@@ -81,8 +81,7 @@
         lax.broadcasted_iota(jnp.int32, (IMAGES, IMAGES), 0)
         == lax.broadcasted_iota(jnp.int32, (IMAGES, IMAGES), 1)
     ).astype(F32)
-    centered = []
-    gram = None
+    blocks = []
     for k in range(NX):
         z0 = got_ref[k * 128 : k * 128 + 64, :].astype(F32)
         z1 = got_ref[k * 128 + 64 : (k + 1) * 128, :].astype(F32)
@@ -90,10 +89,9 @@
         odd = jnp.where(lane_lo, pltpu.roll(z0, 64, 1), z1)
         x = jnp.concatenate([even, odd], axis=0)
         center = jnp.sum(x, axis=0, keepdims=True) / IMAGES
-        x = (x - center).astype(BF16)
-        centered.append(x)
-        part = lax.dot_general(x, x, NT, preferred_element_type=F32)
-        gram = part if gram is None else gram + part
+        blocks.append((x - center).astype(BF16))
+    centered = jnp.concatenate(blocks, axis=1)
+    gram = lax.dot_general(centered, centered, NT, preferred_element_type=F32)
     scaled = gram / (IMAGES - 1)
     ridged = scaled + RIDGE * eye
     parts = split(ridged)
@@ -106,9 +104,10 @@
     high = fine_dot(split(v), split(0.0625 * v - 0.5625 * u))
     lower = (2.25 * eye - 2.4375 * u) + 1.6875 * v + high
     high, low = split(lower / jnp.sqrt(frob))
+    white = jnp.dot(high, centered, preferred_element_type=F32)
+    white = white + jnp.dot(low, centered, preferred_element_type=F32)
     for k in range(NX):
-        white = jnp.dot(high, centered[k], preferred_element_type=F32)
-        turn_ref[k] = white + jnp.dot(low, centered[k], preferred_element_type=F32)
+        turn_ref[k] = white[:, k * 128 : (k + 1) * 128]
         for xs in range(NX):
             rows_ref[pl.ds(xs * 128 + k, 32, stride=4), :] = turn_ref[k, pl.ds(xs, 32, stride=4), :]
     out_ref[...] = rows_ref[...].astype(BF16)

time: 71 us -> 70.9 us (level)
  no operation moved by 1% of the time
where the time goes in v9:
time: 70.9 us; the launch traced here: 70.6 us
  blocking collectives  58.7 us (83%)
  starting transfers between devices  6.78 us (10%)
  Pallas kernels  3.09 us (4%)
  local copies, waits for them, and re-layouts  2 us (3%)
    all_to_all x2, blocking collectives, exchange(): return lax.all_to_all(value, axes, 0, 0, tiled=True)  38.7 us
    all_gather x1, blocking collectives, shards(): kernels = lax.all_gather(chunk, ('y', 'c'))  20 us
    all_to_all x1, starting transfers between devices, exchange(): return lax.all_to_all(value, axes, 0, 0, tiled=True)  6.78 us
    broadcast_in_dim x1, local copies, waits for them, and re-layouts, shards(): spread = jnp.broadcast_to(image[None], (group,) + image.shape)  1.96 us
  transfers between devices with their start and end apart: 1, of which 0 were waited for; matrix products, arithmetic and copies ran while one was open for 0% of the time, Pallas kernels for 0%

profile of v9, /device:TPU:1, one launch (start us, length us, event | category | flops | bytes accessed | tf_op | source)
XLA Modules:
  0.0 70.6 jit_solution(12333329600220152333)
XLA Ops:
  0.0 2.0 %broadcast_in_dim.8 = bf16[8,128,512]{2,1,0:T(8,128)(2,1)} broadcast(bf16[128,512]{1,0:T(8,128)(2,1)} %bitcast.15), dimensions={1,2} | broadcast | bytes 1179648 | tf_op jit(solution)/shard_map/broadcast_in_dim | solution.py:141
  2.0 0.0 copy-start
  2.0 6.8 %all-to-all-start = ((bf16[8,128,512]{2,1,0:T(8,128)(2,1)}), bf16[8,128,512]{2,1,0:T(8,128)(2,1)S(1)}, u32[]{:S(2)}, u32[]{:S(2)}) async-start(bf16[8,128,512]{2,1,0:T(8,128)(2,1)} %broadcast_in_dim.8), calls=%async_computation | async-start | bytes 2097152 | tf_op jit(solution)/shard_map/all_to_all | solution.py:134
  8.7 0.0 copy-done
  8.7 0.0 copy-start.1
  8.8 20.0 %all_gather.3.weight_ref = bf16[16,9,4,512]{3,2,1,0:T(4,128)(2,1)S(1)} all-gather(bf16[1,9,4,512]{3,2,1,0:T(4,128)(2,1)S(1)} %bitcast.16), channel_id=1, replica_groups=mesh['x'=4,'z'=2,'y'=8,'c'=2,'rep'=4] {'y','c'}, dimensions={0}, use_global_device_ids=true | all-gather | bytes 626688 | tf_op jit(solution)/shard_map/all_gather | solution.py:143
  28.8 0.0 copy-done.1
  28.8 0.0 all-to-all-done.image_ref
  28.8 1.3 %shard_map.37 = bf16[512,128]{1,0:T(8,128)(2,1)S(1)} custom-call(bf16[16,9,4,512]{3,2,1,0:T(4,128)(2,1)S(1)} %all_gather.3.weight_ref, bf16[8,128,512]{2,1,0:T(8,128)(2,1)S(1)} %all-to-all-done.image_ref), custom_call_target="tpu_custom_call" | custom-call | tf_op jit(solution)/shard_map/pallas_call | solution.py:146
  30.1 21.6 %all_to_all.15 = bf16[128,4,128]{2,1,0:T(4,128)(2,1)S(1)} all-to-all(bf16[128,4,128]{2,1,0:T(4,128)(2,1)S(1)} %bitcast.10), channel_id=1, replica_groups=mesh['x'=4,'z'=2,'y'=8,'c'=2,'rep'=4] {'x','z','y','c'}, dimensions={0} | all-to-all | bytes 262144 | tf_op jit(solution)/shard_map/all_to_all | solution.py:134
  51.7 0.9 %shard_map.38 = bf16[512,128]{1,0:T(8,128)(2,1)S(1)} custom-call(bf16[512,128]{1,0:T(8,128)(2,1)S(1)} %bitcast.12), custom_call_target="tpu_custom_call" | custom-call | tf_op jit(solution)/shard_map/pallas_call | solution.py:157
  52.6 17.1 %all_to_all.16 = bf16[128,4,128]{2,1,0:T(4,128)(2,1)S(1)} all-to-all(bf16[128,4,128]{2,1,0:T(4,128)(2,1)S(1)} %bitcast.13), channel_id=1, replica_groups=mesh['x'=4,'z'=2,'y'=8,'c'=2,'rep'=4] {'x','z','y','c'}, dimensions={0} | all-to-all | bytes 262144 | tf_op jit(solution)/shard_map/all_to_all | solution.py:134
  69.8 0.8 %shard_map.39 = bf16[128,512]{1,0:T(8,128)(2,1)} custom-call(bf16[512,128]{1,0:T(8,128)(2,1)S(1)} %bitcast.11, f32[9,8,128]{2,1,0:T(8,128)S(1)} %bitcast.14), custom_call_target="tpu_custom_call" | custom-call | tf_op jit(solution)/shard_map/pallas_call | solution.py:163
  (2 shorter events, 0.0 us)
Async XLA Ops:
  2.0 6.8 %copy-start = (bf16[3,3,512,4]{2,3,1,0:T(4,128)(2,1)S(1)}, bf16[3,3,512,4]{2,3,1,0:T(4,128)(2,1)}, u32[]{:S(2)}) copy-start(bf16[3,3,512,4]{2,3,1,0:T(4,128)(2,1)} %param.4) | copy-start | bytes 110596
  2.0 26.8 %all-to-all-start = ((bf16[8,128,512]{2,1,0:T(8,128)(2,1)}), bf16[8,128,512]{2,1,0:T(8,128)(2,1)S(1)}, u32[]{:S(2)}, u32[]{:S(2)}) async-start(bf16[8,128,512]{2,1,0:T(8,128)(2,1)} %broadcast_in_dim.8), calls=%async_computation | async-start | bytes 2097152 | tf_op jit(solution)/shard_map/all_to_all | solution.py:134
  8.7 20.0 %copy-start.1 = (f32[3,3,512]{2,1,0:T(4,128)S(1)}, f32[3,3,512]{2,1,0:T(4,128)}, u32[]{:S(2)}) copy-start(f32[3,3,512]{2,1,0:T(4,128)} %param.5) | copy-start | bytes 55300

commit v10 on v9

--- a/solution.py
+++ b/solution.py
@@ -24,17 +24,15 @@
 
 
 def conv_body(weight_ref, image_ref, out_ref, tall_ref, z_ref, rows_ref):
-    tall_ref[576:640, :] = jnp.zeros((64, CH), F32)
+    group = NX * NZ
     for t in range(9):
-        for g in range(NY * NC):
-            at = t * 64 + g * 4
-            tall_ref[at : at + 4, :] = weight_ref[g, t].astype(F32)
-    group = NX * NZ
+        tall_ref[t * 64 : (t + 1) * 64, :] = weight_ref[:, t].astype(F32).reshape(64, CH).astype(BF16)
+    tall_ref[576:640, :] = jnp.zeros((64, CH), BF16)
     z_ref[:, :, 0:16] = jnp.zeros((5, group, 16, 128), F32)
     z_ref[:, :, 144:160] = jnp.zeros((5, group, 16, 128), F32)
     x = image_ref[...].reshape(group * ROWS * COLS, CH)
     for lo, hi in ((0, 256), (256, 512), (512, 640)):
-        wide = tall_ref[lo:hi, :].astype(BF16)
+        wide = tall_ref[lo:hi, :]
         part = lax.dot_general(x, wide, NT, preferred_element_type=F32)
         for at in range(lo, hi, 128):
             z_ref[at // 128, :, 16:144] = part[:, at - lo : at - lo + 128].reshape(group, 128, 128)
@@ -147,7 +145,7 @@
         conv_body,
         jax.ShapeDtypeStruct((512, 128), BF16),
         [
-            pltpu.VMEM((640, CH), F32),
+            pltpu.VMEM((640, CH), BF16),
             pltpu.VMEM((5, group, 160, 128), F32),
             pltpu.VMEM((512, 128), F32),
         ],

time: 70.9 us -> 70.9 us (level)
  no operation moved by 1% of the time
where the time goes in v10:
time: 70.9 us; the launch traced here: 70.5 us
  blocking collectives  58.7 us (83%)
  starting transfers between devices  6.78 us (10%)
  Pallas kernels  3.03 us (4%)
  local copies, waits for them, and re-layouts  2 us (3%)
    all_to_all x2, blocking collectives, exchange(): return lax.all_to_all(value, axes, 0, 0, tiled=True)  38.7 us
    all_gather x1, blocking collectives, shards(): kernels = lax.all_gather(chunk, ('y', 'c'))  20 us
    all_to_all x1, starting transfers between devices, exchange(): return lax.all_to_all(value, axes, 0, 0, tiled=True)  6.78 us
    broadcast_in_dim x1, local copies, waits for them, and re-layouts, shards(): spread = jnp.broadcast_to(image[None], (group,) + image.shape)  1.96 us
  transfers between devices with their start and end apart: 1, of which 0 were waited for; matrix products, arithmetic and copies ran while one was open for 0% of the time, Pallas kernels for 0%

profile of v10, /device:TPU:1, one launch (start us, length us, event | category | flops | bytes accessed | tf_op | source)
XLA Modules:
  0.0 70.5 jit_solution(17779801900231774732)
XLA Ops:
  0.0 2.0 %broadcast_in_dim.8 = bf16[8,128,512]{2,1,0:T(8,128)(2,1)} broadcast(bf16[128,512]{1,0:T(8,128)(2,1)} %bitcast.15), dimensions={1,2} | broadcast | bytes 1179648 | tf_op jit(solution)/shard_map/broadcast_in_dim | solution.py:139
  2.0 0.0 copy-start
  2.0 6.8 %all-to-all-start = ((bf16[8,128,512]{2,1,0:T(8,128)(2,1)}), bf16[8,128,512]{2,1,0:T(8,128)(2,1)S(1)}, u32[]{:S(2)}, u32[]{:S(2)}) async-start(bf16[8,128,512]{2,1,0:T(8,128)(2,1)} %broadcast_in_dim.8), calls=%async_computation | async-start | bytes 2097152 | tf_op jit(solution)/shard_map/all_to_all | solution.py:132
  8.7 0.0 copy-done
  8.7 0.0 copy-start.1
  8.8 20.0 %all_gather.3.weight_ref = bf16[16,9,4,512]{3,2,1,0:T(4,128)(2,1)S(1)} all-gather(bf16[1,9,4,512]{3,2,1,0:T(4,128)(2,1)S(1)} %bitcast.16), channel_id=1, replica_groups=mesh['x'=4,'z'=2,'y'=8,'c'=2,'rep'=4] {'y','c'}, dimensions={0}, use_global_device_ids=true | all-gather | bytes 626688 | tf_op jit(solution)/shard_map/all_gather | solution.py:141
  28.8 0.0 copy-done.1
  28.8 0.0 all-to-all-done.image_ref
  28.8 1.2 %shard_map.37 = bf16[512,128]{1,0:T(8,128)(2,1)S(1)} custom-call(bf16[16,9,4,512]{3,2,1,0:T(4,128)(2,1)S(1)} %all_gather.3.weight_ref, bf16[8,128,512]{2,1,0:T(8,128)(2,1)S(1)} %all-to-all-done.image_ref), custom_call_target="tpu_custom_call" | custom-call | tf_op jit(solution)/shard_map/pallas_call | solution.py:144
  30.0 21.6 %all_to_all.15 = bf16[128,4,128]{2,1,0:T(4,128)(2,1)S(1)} all-to-all(bf16[128,4,128]{2,1,0:T(4,128)(2,1)S(1)} %bitcast.10), channel_id=1, replica_groups=mesh['x'=4,'z'=2,'y'=8,'c'=2,'rep'=4] {'x','z','y','c'}, dimensions={0} | all-to-all | bytes 262144 | tf_op jit(solution)/shard_map/all_to_all | solution.py:132
  51.6 0.9 %shard_map.38 = bf16[512,128]{1,0:T(8,128)(2,1)S(1)} custom-call(bf16[512,128]{1,0:T(8,128)(2,1)S(1)} %bitcast.12), custom_call_target="tpu_custom_call" | custom-call | tf_op jit(solution)/shard_map/pallas_call | solution.py:155
  52.6 17.1 %all_to_all.16 = bf16[128,4,128]{2,1,0:T(4,128)(2,1)S(1)} all-to-all(bf16[128,4,128]{2,1,0:T(4,128)(2,1)S(1)} %bitcast.13), channel_id=1, replica_groups=mesh['x'=4,'z'=2,'y'=8,'c'=2,'rep'=4] {'x','z','y','c'}, dimensions={0} | all-to-all | bytes 262144 | tf_op jit(solution)/shard_map/all_to_all | solution.py:132
  69.7 0.8 %shard_map.39 = bf16[128,512]{1,0:T(8,128)(2,1)} custom-call(bf16[512,128]{1,0:T(8,128)(2,1)S(1)} %bitcast.11, f32[9,8,128]{2,1,0:T(8,128)S(1)} %bitcast.14), custom_call_target="tpu_custom_call" | custom-call | tf_op jit(solution)/shard_map/pallas_call | solution.py:161
  (2 shorter events, 0.0 us)
Async XLA Ops:
  2.0 6.8 %copy-start = (bf16[3,3,512,4]{2,3,1,0:T(4,128)(2,1)S(1)}, bf16[3,3,512,4]{2,3,1,0:T(4,128)(2,1)}, u32[]{:S(2)}) copy-start(bf16[3,3,512,4]{2,3,1,0:T(4,128)(2,1)} %param.4) | copy-start | bytes 110596
  2.0 26.8 %all-to-all-start = ((bf16[8,128,512]{2,1,0:T(8,128)(2,1)}), bf16[8,128,512]{2,1,0:T(8,128)(2,1)S(1)}, u32[]{:S(2)}, u32[]{:S(2)}) async-start(bf16[8,128,512]{2,1,0:T(8,128)(2,1)} %broadcast_in_dim.8), calls=%async_computation | async-start | bytes 2097152 | tf_op jit(solution)/shard_map/all_to_all | solution.py:132
  8.7 20.0 %copy-start.1 = (f32[3,3,512]{2,1,0:T(4,128)S(1)}, f32[3,3,512]{2,1,0:T(4,128)}, u32[]{:S(2)}) copy-start(f32[3,3,512]{2,1,0:T(4,128)} %param.5) | copy-start | bytes 55300
